TPU v7x, 32 devices: a whole 2x2x4 slice. The times are simulated.
32 devices in a mesh: gx: 4 (over y, x), gy: 4 (over z), gz: 2 (over core).
Axes of the slice: x: 2, y: 2, z: 4, core: 2. Of those that a mesh axis runs over, the one named last changes fastest.
Arguments:
- state: float32 [3, 32, 160, 512], P(None, 'gz', 'gy', 'gx'), may hold values from -6 to 6
- right_side: float32 [3, 32, 160, 512], P(None, 'gz', 'gy', 'gx'), may hold values from -6 to 6
- permeability: bfloat16 [32, 160, 512], P('gz', 'gy', 'gx'), may hold values from 0.099609375 to 10
- pore_volume: bfloat16 [32, 160, 512], P('gz', 'gy', 'gx'), may hold values from 0.019897461 to 0.19921875
- facies: int32 [32], P('gz'), may hold values from 0 to 3
- storage_table: float32 [4, 3, 3], replicated, may hold values from -0.3 to 2, as said below
- coupling_table: float32 [4, 3, 3], replicated, may hold values from -0.3 to 2, as said below
Outputs:
- new_state: float32 [3, 32, 160, 512], P(None, 'gz', 'gy', 'gx')
- correction: float32 [160, 512], P('gy', 'gx')
Inputs may be any that keep to these rules, and one draw needn't show every extreme that they name: `storage_table`: each facies block has a diagonal of 1 to 2 and off-diagonal entries of magnitude at most 0.3. `coupling_table`: each facies block has a diagonal of 1 to 2 and off-diagonal entries of magnitude at most 0.3.
All inputs are finite; a program needn't handle non-finite values.
Results may differ from a plain program's by a relative error of at most 0.0003.
Values sent between devices are 32-bit elements; how exact they have to be, the bound alone decides.
A program may use at most 64 MiB of HBM per device.

v0:
```python
import functools
import jax
import jax.numpy as jnp
from jax import lax
from jax.experimental import pallas as pl
from jax.experimental.pallas import tpu as pltpu
from jax.sharding import PartitionSpec as P

SWEEPS = 8
RELAX = 0.8
MESH = pl.DeviceIdType.MESH
HALO = 8
VMEM_BYTES = 67043328

PLANES = 4
SIDES = [(-1, 0), (1, 0), (0, -1), (0, 1), (-1, -1), (-1, 1), (1, -1), (1, 1)]

KINV, NMAT, NADJ, NDIA, NTR, NC2, NDET, NCOEF = 0, 9, 18, 27, 30, 31, 32, 33


def cofactor(e, r, c):
    return (e[(r + 1) % 3][(c + 1) % 3] * e[(r + 2) % 3][(c + 2) % 3]
            - e[(r + 1) % 3][(c + 2) % 3] * e[(r + 2) % 3][(c + 1) % 3])


def block_scalars(m, k):
    kf = [[cofactor(k, r, c) for c in range(3)] for r in range(3)]
    inv = 1.0 / (k[0][0] * kf[0][0] + k[0][1] * kf[0][1] + k[0][2] * kf[0][2])
    kinv = [[kf[c][r] * inv for c in range(3)] for r in range(3)]
    n = [[kinv[r][0] * m[0][c] + kinv[r][1] * m[1][c] + kinv[r][2] * m[2][c] for c in range(3)] for r in range(3)]
    nf = [[cofactor(n, r, c) for c in range(3)] for r in range(3)]
    trace = n[0][0] + n[1][1] + n[2][2]
    return ([kinv[r][c] for r in range(3) for c in range(3)] + [n[r][c] for r in range(3) for c in range(3)]
            + [nf[c][r] for r in range(3) for c in range(3)] + [trace - n[i][i] for i in range(3)]
            + [trace, nf[0][0] + nf[1][1] + nf[2][2], n[0][0] * nf[0][0] + n[0][1] * nf[0][1] + n[0][2] * nf[0][2]])


def column_plan(nz, ny, nx):
    groups = ny // HALO
    per = nx // (2 * nz)
    return groups, per, -(-groups // per)


def strip_plan(ny, nx):
    groups = ny // HALO
    per = nx // (2 * HALO * PLANES)
    heads = [0] if groups == 1 else [0, groups - 1]
    others = list(range(1, groups - 1))
    packed = [[head] + [others.pop(0) for _ in range(per - 1) if others] for head in heads]
    while others:
        packed.append([others.pop(0) for _ in range(per) if others])
    return packed


def kernel(sizes, facies_hbm, mtab_hbm, ktab_hbm, state_hbm, rhs_hbm, perm_hbm, pore_hbm,
           w, qv, tzs, ty, txp, txm, final,
           u, pcb, rhs, permb, poreb, ysend, yrecv, xsend, xrecv, edge, rowk, tzf, shifted,
           zplanes, strips, cyrecv, cxrecv, cdrecv, field,
           facies, mtab, ktab, ctab, near_sem, far_sem, in_sem, h_send, h_recv, c_send, c_recv):
    ngx, ngy, ngz, nz, ny, nx = sizes
    ix, iy, iz = lax.axis_index("gx"), lax.axis_index("gy"), lax.axis_index("gz")
    own = slice(HALO, HALO + ny)
    groups, per, xtiles = column_plan(nz, ny, nx)
    packing = strip_plan(ny, nx)
    f32 = jnp.float32

    def exists(dy, dx):
        ok = None
        for d, i, n in ((dy, iy, ngy), (dx, ix, ngx)):
            if d:
                here = (i > 0) if d < 0 else (i < n - 1)
                ok = here if ok is None else jnp.logical_and(ok, here)
        return ok

    def at(dy, dx):
        return {"gx": ix + dx, "gy": iy + dy, "gz": iz}

    barrier = pltpu.get_barrier_semaphore()
    for side in SIDES[:4]:
        @pl.when(exists(*side))
        def _(side=side):
            pl.semaphore_signal(barrier, inc=1, device_id=at(*side), device_id_type=MESH)

    def signal_peers(sem):
        for d in range(1, ngz):
            pl.semaphore_signal(sem, inc=1, device_id={"gx": ix, "gy": iy, "gz": lax.rem(iz + d, ngz)},
                                device_id_type=MESH)

    signal_peers(barrier)

    loads = [
        pltpu.make_async_copy(perm_hbm, permb, in_sem.at[0]),
        pltpu.make_async_copy(state_hbm, u.at[0:3, 1:nz + 1, own], in_sem.at[1]),
        pltpu.make_async_copy(pore_hbm, poreb, in_sem.at[2]),
        pltpu.make_async_copy(rhs_hbm, rhs, in_sem.at[3]),
        pltpu.make_async_copy(facies_hbm, facies, in_sem.at[4]),
        pltpu.make_async_copy(mtab_hbm, mtab, in_sem.at[5]),
        pltpu.make_async_copy(ktab_hbm, ktab, in_sem.at[6]),
    ]
    for i in (4, 6, 5, 0, 1, 2, 3):
        loads[i].start()

    def zero(ref):
        ref[...] = jnp.zeros(ref.shape, ref.dtype)

    for cond, refs in (
        (iz == 0, [u.at[:, 0, own]]),
        (iz == ngz - 1, [u.at[:, nz + 1, own]]),
        (iy == 0, [yrecv.at[:, 0], cyrecv.at[0]]),
        (iy == ngy - 1, [yrecv.at[:, 1], cyrecv.at[1]]),
        (ix == 0, [xrecv.at[:, 0], cxrecv.at[0]]),
        (ix == ngx - 1, [xrecv.at[:, 1], cxrecv.at[1]]),
        (jnp.logical_or(iy == 0, ix == 0), [cdrecv.at[0]]),
        (jnp.logical_or(iy == 0, ix == ngx - 1), [cdrecv.at[1]]),
        (jnp.logical_or(iy == ngy - 1, ix == 0), [cdrecv.at[2]]),
        (jnp.logical_or(iy == ngy - 1, ix == ngx - 1), [cdrecv.at[3]]),
    ):
        @pl.when(cond)
        def _(refs=refs):
            for ref in refs:
                zero(ref)
    zero(field)
    for z in range(nz):
        zero(pcb.at[z, HALO + ny:])
    zero(shifted.at[:, 0:HALO])

    for i in (4, 6, 5):
        loads[i].wait()

    def coefficient(table, z, r, c):
        return table[r, facies[z], c]

    lane8 = lax.broadcasted_iota(jnp.int32, (HALO, nx), 1)
    row8 = lax.broadcasted_iota(jnp.int32, (HALO, nx), 0)
    pair8 = lax.shift_right_logical(lane8, 1)
    even8 = lax.rem(lane8, 2) == 0
    first8, last8 = lane8 == 0, lane8 == nx - 1
    nil8 = jnp.zeros((HALO, nx), f32)

    for f in range(ktab.shape[1]):
        values = block_scalars([[mtab[r, f, c] for c in range(3)] for r in range(3)],
                               [[ktab[r, f, c] for c in range(3)] for r in range(3)])
        for i, value in enumerate(values):
            ctab[i, f] = value
    layer_of_lane = lax.rem(lane8[0:1], 2 * nz) // 2
    lanek = [jnp.zeros((1, nx), f32) for _ in range(3)]
    for z in range(nz):
        for k in range(3):
            value = coefficient(ktab, z, 0, k)
            rowk[k, z:z + 1, :] = jnp.full((1, nx), value, f32)
            lanek[k] = jnp.where(layer_of_lane == z, value, lanek[k])

    def packed_columns(values):
        out = [nil8] * xtiles
        for z, g, x in values:
            place = (g % per) * nz + z
            out[g // per] = jnp.where(pair8 == place, pltpu.roll(x, 2 * place + 1, 1), out[g // per])
        return out

    def swapped(x):
        return jnp.where(even8, pltpu.roll(x, nx - 1, 1), pltpu.roll(x, 1, 1))

    loads[0].wait()
    values = []
    for z in range(nz):
        r = 0.5 / permb[z].astype(f32)
        u[3, z + 1, own, :] = r
        for side, at_row in ((0, 0), (1, ny - 1)):
            ysend[0, side, nz + z:nz + z + 1, :] = r[at_row:at_row + 1]
        values += [(z, g, r[g * HALO:(g + 1) * HALO]) for g in range(groups)]
    packed = packed_columns(values)
    for t in range(xtiles):
        xsend[0, 1, t] = packed[t]

    loads[1].wait()
    values = []
    for z in range(nz):
        k0 = [coefficient(ktab, z, 0, k) for k in range(3)]
        pc = k0[0] * u[0, z + 1, own, :] + k0[1] * u[1, z + 1, own, :] + k0[2] * u[2, z + 1, own, :]
        pcb[z, own, :] = pc
        for side, at_row in ((0, 0), (1, ny - 1)):
            ysend[0, side, z:z + 1, :] = pc[at_row:at_row + 1]
        values += [(z, g, pc[g * HALO:(g + 1) * HALO]) for g in range(groups)]
    packed = packed_columns(values)
    for t in range(xtiles):
        xsend[0, 0, t] = packed[t]

    beside_y = exists(-1, 0).astype(jnp.int32) + exists(1, 0).astype(jnp.int32)
    beside_x = exists(0, -1).astype(jnp.int32) + exists(0, 1).astype(jnp.int32)
    pl.semaphore_wait(barrier, beside_y + beside_x + (ngz - 1))

    def remote(src, dst, send, recv, device):
        return pltpu.make_async_remote_copy(src_ref=src, dst_ref=dst, send_sem=send, recv_sem=recv,
                                            device_id=device, device_id_type=MESH)

    def start(copies):
        for sends, copy in copies:
            @pl.when(sends)
            def _(copy=copy):
                copy.start()

    def y_copies(batch):
        s = h_send.at[2 + batch], h_recv.at[2 + batch]
        return [(exists(1, 0), remote(ysend.at[batch, 1], yrecv.at[batch, 0], *s, at(1, 0))),
                (exists(-1, 0), remote(ysend.at[batch, 0], yrecv.at[batch, 1], *s, at(-1, 0)))]

    def x_copies(batch):
        s = h_send.at[4 + batch], h_recv.at[4 + batch]
        return [(exists(0, 1), remote(xsend.at[batch], xrecv.at[batch, 0], *s, at(0, 1))),
                (exists(0, -1), remote(xsend.at[batch], xrecv.at[batch, 1], *s, at(0, -1)))]

    def z_device(d):
        return {"gx": ix, "gy": iy, "gz": iz + d}

    z_up = remote(u.at[:, nz, own], u.at[:, 0, own], h_send.at[0], h_recv.at[0], z_device(1))
    z_down = remote(u.at[:, 1, own], u.at[:, nz + 1, own], h_send.at[1], h_recv.at[1], z_device(-1))
    has_below, has_above = iz > 0, iz < ngz - 1

    start(x_copies(0))
    start(y_copies(0))
    start([(has_above, z_up), (has_below, z_down)])
    for side in SIDES[:4]:
        @pl.when(exists(*side))
        def _(side=side):
            pl.semaphore_signal(near_sem, inc=1, device_id=at(*side), device_id_type=MESH)
    signal_peers(near_sem)

    def counted(count, cases, descriptor, done):
        for n, ref in cases:
            @pl.when(count == n)
            def _(ref=ref):
                done(descriptor(ref))

    def wait_many(count, cases, send, recv, sent):
        counted(count, cases, lambda ref: remote(ref, ref, send, recv, z_device(0)),
                (lambda c: c.wait_send()) if sent else (lambda c: c.wait_recv()))

    def wait_y(batch, sent):
        wait_many(beside_y, ((1, yrecv.at[batch, 0]), (2, yrecv.at[batch])), h_send.at[2 + batch], h_recv.at[2 + batch], sent)

    def wait_x(batch, sent):
        wait_many(beside_x, ((1, xrecv.at[batch, 0]), (2, xrecv.at[batch])), h_send.at[4 + batch], h_recv.at[4 + batch], sent)

    for i in range(2):
        values = []
        for z in range(nz):
            c = u[1 + i, z + 1, own, :]
            for side, at_row in ((0, 0), (1, ny - 1)):
                ysend[1, side, i * nz + z:i * nz + z + 1, :] = c[at_row:at_row + 1]
            values += [(z, g, c[g * HALO:(g + 1) * HALO]) for g in range(groups)]
        packed = packed_columns(values)
        for t in range(xtiles):
            xsend[1, i, t] = packed[t]
    start(x_copies(1))
    start(y_copies(1))

    loads[2].wait()
    loads[3].wait()

    def tile_of(g):
        return slice(g * HALO, (g + 1) * HALO)

    def padded(g, shift):
        return slice(HALO + g * HALO + shift, HALO + (g + 1) * HALO + shift)

    def assemble(z, carry, upper=True):
        s_res, s_dia, s_ty, s_tx, s_hx, s_hy, s_z = (list(c) for c in carry)
        volume = poreb[z].astype(f32)
        k00 = coefficient(ktab, z, 0, 0)
        m0 = [coefficient(mtab, z, 0, k) for k in range(3)]
        if upper:
            dk = [coefficient(ktab, z, 0, k) - coefficient(ktab, z + 1, 0, k) for k in range(3)]
        for g in range(groups):
            rows = padded(g, 0)
            r = u[3, z + 1, rows, :]
            typ = 1.0 / (r + u[3, z + 1, padded(g, 1), :])
            if g == groups - 1:
                typ = jnp.where(row8 < HALO - 1, typ, 0.0)
            xp = jnp.where(last8, 0.0, 1.0 / (r + pltpu.roll(r, nx - 1, 1)))
            ty[z, rows, :] = typ
            txp[z, tile_of(g), :] = xp
            pc = pcb[z, rows, :]
            s_hx[g] = s_hx[g] + xp * (pc - pltpu.roll(pc, nx - 1, 1))
            s_hy[g] = s_hy[g] + typ * (pc - pcb[z, padded(g, 1), :])
            v = volume[tile_of(g)]
            c = [u[k, z + 1, rows, :] for k in range(3)]
            s_res[g] = s_res[g] + (rhs[0, z, tile_of(g), :] - v * (m0[0] * c[0] + m0[1] * c[1] + m0[2] * c[2]))
            s_dia[g] = s_dia[g] + v * m0[0]
            s_ty[g] = s_ty[g] + k00 * typ
            s_tx[g] = s_tx[g] + k00 * xp
            if upper:
                t = 1.0 / (r + u[3, z + 2, rows, :])
                tzf[z + 1, tile_of(g), :] = t
                d = [c[k] - u[k, z + 2, rows, :] for k in range(3)]
                s_z[g] = s_z[g] + t * (dk[0] * d[0] + dk[1] * d[1] + dk[2] * d[2])
        return tuple(tuple(s) for s in (s_res, s_dia, s_ty, s_tx, s_hx, s_hy, s_z))

    carry = ((nil8,) * groups,) * 7
    trips = (nz - 1) // 2

    def two(i, carry):
        return assemble(2 * i + 1, assemble(2 * i, carry))

    carry = lax.fori_loop(0, trips, two, carry)
    for z in range(2 * trips, nz):
        carry = assemble(z, carry, upper=z < nz - 1)
    s_res, s_dia, s_ty, s_tx, s_hx, s_hy, s_z = (list(c) for c in carry)

    for g in range(groups):
        shifted[0, padded(g, 0), :] = s_hy[g]
        shifted[1, padded(g, 0), :] = s_ty[g]
    p_rhs, p_dia = [], []
    for g in range(groups):
        p_rhs.append(s_res[g] - s_z[g] - (s_hx[g] - pltpu.roll(s_hx[g], 1, 1)) - (s_hy[g] - shifted[0, padded(g, -1), :]))
        p_dia.append(s_dia[g] + s_ty[g] + shifted[1, padded(g, -1), :] + s_tx[g] + pltpu.roll(s_tx[g], 1, 1))

    @pl.when(has_below)
    def _():
        z_up.wait_recv()

    @pl.when(has_above)
    def _():
        z_down.wait_recv()
    for slot, z, inside in ((0, 0, 1), (nz + 1, nz - 1, nz)):
        k0 = [coefficient(ktab, z, 0, k) for k in range(3)]
        for g in range(groups):
            rows = padded(g, 0)
            there = u[3, slot, rows, :]
            t = jnp.where(there > 0.0, 1.0 / (u[3, inside, rows, :] + there), 0.0)
            tzf[0 if slot == 0 else nz, tile_of(g), :] = t
            d = [u[k, inside, rows, :] - u[k, slot, rows, :] for k in range(3)]
            p_rhs[g] = p_rhs[g] - t * (k0[0] * d[0] + k0[1] * d[1] + k0[2] * d[2])
    mine = [[swapped(xsend[0, i, t]) for t in range(xtiles)] for i in range(2)]
    pl.semaphore_wait(near_sem, beside_y + beside_x + (ngz - 1))
    signal_peers(far_sem)

    wait_y(0, False)
    for side, at_row, g in ((0, 0, 0), (1, HALO - 1, groups - 1)):
        there = yrecv[0, side, nz:, :]
        t = jnp.where(there > 0.0, 1.0 / (ysend[0, side, nz:, :] + there), 0.0)
        for z in range(nz):
            edge_row = HALO - 1 + side * ny
            ty[z, edge_row:edge_row + 1, :] = t[z:z + 1]
        moved = jnp.sum(t * (ysend[0, side, :nz, :] - yrecv[0, side, :nz, :]), axis=0, keepdims=True)
        weight = jnp.sum(rowk[0] * t, axis=0, keepdims=True)
        here = row8 == at_row
        p_rhs[g] = p_rhs[g] - jnp.where(here, moved, 0.0)
        p_dia[g] = p_dia[g] + jnp.where(here, weight, 0.0)
        if side:
            s_ty[g] = s_ty[g] + jnp.where(here, weight, 0.0)
    planes = [p_rhs, p_dia, s_ty, s_tx]
    group8 = lax.shift_right_logical(lane8, 4)
    packed = []
    for tiles in packing:
        strip = nil8
        for i, g in enumerate(tiles):
            for p in range(PLANES):
                slot = i * PLANES + p
                strip = jnp.where(group8 == slot, pltpu.roll(planes[p][g], (2 * HALO * slot + HALO) % nx, 1), strip)
        packed.append(strip)

    wait_x(0, False)
    flux, weights, faces, outside = [], [], [], []
    for t in range(xtiles):
        there = [jnp.where(even8, xrecv[0, 0, i, t], xrecv[0, 1, i, t]) for i in range(2)]
        face = jnp.where(there[1] > 0.0, 1.0 / (mine[1][t] + there[1]), 0.0)
        flux.append(face * (mine[0][t] - there[0]))
        weights.append(face * lanek[0])
        faces.append(face)
        outside.append(there[0])
    in16 = lax.rem(lane8, 2 * HALO)
    for i, tiles in enumerate(packing):
        for j, g in enumerate(tiles):
            low = (g % per) * 2 * nz
            block = jnp.logical_and(lane8 >= low, lane8 < low + 2 * nz)
            sums = []
            for values in (flux, weights):
                for parity in (even8, jnp.logical_not(even8)):
                    chosen = jnp.where(jnp.logical_and(block, parity), values[g // per], 0.0)
                    sums.append(jnp.sum(chosen, axis=1, keepdims=True))
            for p, left, right, sign in ((0, sums[0], sums[1], -1.0), (1, sums[2], sums[3], 1.0), (3, None, sums[3], 1.0)):
                slot = (j * PLANES + p) * 2 * HALO
                at_left, at_right = lane8 == slot + HALO, lane8 == slot + HALO - 1
                change = jnp.where(last8, sign * right, 0.0)
                moved = jnp.where(at_right, sign * right, 0.0)
                if left is not None:
                    change = jnp.where(first8, sign * left, change)
                    moved = jnp.where(at_left, sign * left, moved)
                planes[p][g] = planes[p][g] + change
                packed[i] = packed[i] + moved
    for i in range(len(packing)):
        strips[i] = packed[i]
    for p in range(PLANES):
        for g in range(groups):
            zplanes[iz, p, tile_of(g), :] = planes[p][g]

    pl.semaphore_wait(far_sem, ngz - 1)
    copies = []
    for n, (dy, dx) in enumerate(SIDES[4:]):
        into = (1 - dy) + (1 - dx) // 2
        src = strips.at[0 if dy < 0 or len(packing) == 1 else 1]
        for d in range(ngz):
            device = {"gx": ix + dx, "gy": iy + dy, "gz": lax.rem(iz + d, ngz)}
            copies.append((exists(dy, dx), remote(src, cdrecv.at[into, iz], c_send.at[3], c_recv.at[3], device)))
    for dx in (-1, 1):
        for d in range(ngz):
            device = {"gx": ix + dx, "gy": iy, "gz": lax.rem(iz + d, ngz)}
            copies.append((exists(0, dx), remote(strips, cxrecv.at[(1 - dx) // 2, iz], c_send.at[2], c_recv.at[2], device)))
    for dy in (-1, 1):
        src = zplanes.at[iz, :, 0:HALO] if dy < 0 else zplanes.at[iz, :, ny - HALO:ny]
        for d in range(ngz):
            device = {"gx": ix, "gy": iy + dy, "gz": lax.rem(iz + d, ngz)}
            copies.append((exists(dy, 0), remote(src, cyrecv.at[(1 - dy) // 2, iz], c_send.at[1], c_recv.at[1], device)))
    start(copies)
    for d in range(1, ngz):
        remote(zplanes.at[iz], zplanes.at[iz], c_send.at[0], c_recv.at[0],
               {"gx": ix, "gy": iy, "gz": lax.rem(iz + d, ngz)}).start()

    wait_y(1, False)
    wait_x(1, False)
    invrow = 1.0 / rowk[0]
    for side, at_row in ((0, HALO - 1), (1, HALO + ny)):
        one, two_ = yrecv[1, side, :nz, :], yrecv[1, side, nz:, :]
        zero_ = (yrecv[0, side, :nz, :] - rowk[1] * one - rowk[2] * two_) * invrow
        for z in range(nz):
            for k, x in enumerate((zero_, one, two_)):
                u[k, z + 1, at_row:at_row + 1, :] = x[z:z + 1]
    invlane = 1.0 / lanek[0]
    for t in range(xtiles):
        one, two_ = (jnp.where(even8, xrecv[1, 0, i, t], xrecv[1, 1, i, t]) for i in range(2))
        zero_ = (outside[t] - lanek[1] * one - lanek[2] * two_) * invlane
        for k, x in enumerate((zero_, one, two_)):
            edge[k, t] = swapped(faces[t] * x)
        edge[3, t] = swapped(faces[t])

    outer8 = jnp.logical_or(first8, last8)

    def solve(z, _):
        volume = poreb[z].astype(f32)
        f = facies[z]
        kinv = [[ctab[KINV + 3 * r + c, f] for c in range(3)] for r in range(3)]
        n = [[ctab[NMAT + 3 * r + c, f] for c in range(3)] for r in range(3)]
        adj = [[ctab[NADJ + 3 * r + c, f] for c in range(3)] for r in range(3)]
        dia = [ctab[NDIA + i, f] for i in range(3)]
        trace, minors, det_n = ctab[NTR, f], ctab[NC2, f], ctab[NDET, f]
        for g in range(groups):
            rows = padded(g, 0)
            tile = tile_of(g)
            shift = lax.rem(2 * nx - (2 * nz * (g % per) + 1) - 2 * z, nx)
            lateral = [jnp.where(outer8, pltpu.roll(edge[k, g // per], shift, 1), 0.0) for k in range(4)]
            tzm, tzp = tzf[z, tile, :], tzf[z + 1, tile, :]
            typ, tym = ty[z, rows, :], ty[z, padded(g, -1), :]
            xp = txp[z, tile, :]
            xm = pltpu.roll(xp, 1, 1)
            tz = tzm + tzp
            tzs[z, tile, :] = tz
            total = tz + (typ + tym) + (xp + xm) + lateral[3]
            txp[z, tile, :] = xp + jnp.where(last8, lateral[3], 0.0)
            txm[z, tile, :] = xm + jnp.where(first8, lateral[3], 0.0)
            near = []
            for k in range(3):
                c = u[k, z + 1, rows, :]
                near.append(tzp * u[k, z + 2, rows, :] + tzm * u[k, z, rows, :]
                            + typ * u[k, z + 1, padded(g, 1), :] + tym * u[k, z + 1, padded(g, -1), :]
                            + xp * pltpu.roll(c, nx - 1, 1) + xm * pltpu.roll(c, 1, 1) + lateral[k])
            given = [rhs[k, z, tile, :] for k in range(3)]
            b = [near[r] + kinv[r][0] * given[0] + kinv[r][1] * given[1] + kinv[r][2] * given[2] for r in range(3)]
            v = volume[tile]
            s = total * (1.0 / v)
            e = [[s * (s + dia[r]) + adj[r][r] if r == c else adj[r][c] - s * n[r][c] for c in range(3)] for r in range(3)]
            det = ((s + trace) * s + minors) * s + det_n
            inv = 1.0 / (v * det)
            for r in range(3):
                w[r, z, tile, :] = (e[r][0] * b[0] + e[r][1] * b[1] + e[r][2] * b[2]) * inv
                qv[r, z, tile, :] = e[r][0] * inv
        return 0

    def solve_two(i, carry):
        return solve(2 * i + 1, solve(2 * i, carry))

    lax.fori_loop(0, nz // 2, solve_two, 0)
    if nz % 2:
        solve(nz - 1, 0)

    corners = beside_y * beside_x
    if ngz > 1:
        others = zplanes.at[0:ngz - 1]
        remote(others, others, c_send.at[0], c_recv.at[0], z_device(0)).wait_recv()
    y_cases = ((1, cyrecv.at[0]), (2, cyrecv))
    x_cases = ((1, cxrecv.at[0]), (2, cxrecv))
    d_cases = ((1, cdrecv.at[0]), (2, cdrecv.at[0:2]), (4, cdrecv))
    wait_many(beside_y, y_cases, c_send.at[1], c_recv.at[1], False)
    wait_many(beside_x, x_cases, c_send.at[2], c_recv.at[2], False)
    wait_many(corners, d_cases, c_send.at[3], c_recv.at[3], False)

    def gathered(ref, *index):
        total = ref[index[0], 0] if not index[1:] else ref[(index[0], 0) + index[1:]]
        for i in range(1, ngz):
            total = total + (ref[index[0], i] if not index[1:] else ref[(index[0], i) + index[1:]])
        return total

    rows = ny + 2 * HALO
    elane = lax.broadcasted_iota(jnp.int32, (rows, nx), 1)
    efirst, elast = elane == 0, elane == nx - 1
    left_part = in16 < HALO
    side_tiles = [jnp.where(left_part, gathered(cxrecv, 0, i), gathered(cxrecv, 1, i)) for i in range(len(packing))]
    corner_tiles = [jnp.where(left_part, gathered(cdrecv, 2 * v), gathered(cdrecv, 2 * v + 1)) for v in range(2)]
    where_is = {g: (i, j) for i, tiles in enumerate(packing) for j, g in enumerate(tiles)}
    strip8 = jnp.logical_or(lane8 < HALO, lane8 >= nx - HALO)

    def border_of(p, g):
        if 0 <= g < groups:
            i, j = where_is[g]
            tile, slot = side_tiles[i], j * PLANES + p
        else:
            tile, slot = corner_tiles[0 if g < 0 else 1], p
        return jnp.where(strip8, pltpu.roll(tile, (2 * nx - 2 * HALO * slot - HALO) % nx, 1), 0.0)

    b = [jnp.concatenate([border_of(p, g) for g in range(-1, groups + 1)], axis=0) for p in range(PLANES)]
    a = []
    for p in range(PLANES):
        plane = zplanes[0, p]
        for i in range(1, ngz):
            plane = plane + zplanes[i, p]
        a.append(jnp.concatenate([gathered(cyrecv, 0, p), plane, gathered(cyrecv, 1, p)], axis=0))

    def east(a, b):
        ra, rb = pltpu.roll(a, nx - 1, 1), pltpu.roll(b, nx - 1, 1)
        return jnp.where(elast, rb, ra), jnp.where(elast, ra, rb)

    def west(a, b):
        ra, rb = pltpu.roll(a, 1, 1), pltpu.roll(b, 1, 1)
        return jnp.where(efirst, rb, ra), jnp.where(efirst, ra, rb)

    mid = slice(HALO, HALO + rows)
    wests = west(a[3], b[3])
    terms = []
    for s, planes_ in enumerate((a, b)):
        there = planes_[1] > 0.0
        inv = jnp.where(there, RELAX / jnp.where(there, planes_[1], 1.0), 0.0)
        field[s, mid, :] = planes_[2]
        south = field[s, HALO - 1:HALO - 1 + rows, :]
        terms.append((planes_[0] * inv, planes_[2] * inv, south * inv, planes_[3] * inv, wests[s] * inv))

    c = [terms[0][0], terms[1][0]]
    for sweep in range(1, SWEEPS):
        e, ws = east(*c), west(*c)
        for s in range(2):
            field[s, mid, :] = c[s]
        nxt = []
        for s in range(2):
            r, tyn, tys, txe, txw = terms[s]
            nxt.append((1.0 - RELAX) * c[s] + r
                       + tyn * field[s, HALO + 1:HALO + 1 + rows, :] + tys * field[s, HALO - 1:HALO - 1 + rows, :]
                       + txe * e[s] + txw * ws[s])
        c = nxt
    e, ws = east(*c), west(*c)
    final[0] = c[0]
    final[1] = e[0]
    final[2] = ws[0]
    @pl.when(has_above)
    def _():
        z_up.wait_send()

    @pl.when(has_below)
    def _():
        z_down.wait_send()
    for batch in range(2):
        wait_y(batch, True)
        wait_x(batch, True)
    if ngz > 1:
        remote(others, others, c_send.at[0], c_recv.at[0], z_device(0)).wait_send()
    wait_many(beside_y, y_cases, c_send.at[1], c_recv.at[1], True)
    wait_many(beside_x, x_cases, c_send.at[2], c_recv.at[2], True)
    wait_many(corners, d_cases, c_send.at[3], c_recv.at[3], True)


def finish_kernel(parts, w, qv, tzs, ty, txp, txm, final, new_hbm, corr_hbm, out, out_sem):
    nz, ny, nx = tzs.shape
    own = slice(HALO, HALO + ny)
    corr = pltpu.make_async_copy(final.at[0, own], corr_hbm, out_sem.at[parts])
    corr.start()
    cc, ce, cw = (final[k, own, :] for k in range(3))
    cn, cs = final[0, HALO + 1:HALO + 1 + ny, :], final[0, HALO - 1:HALO - 1 + ny, :]

    def finish(z, _):
        g = (tzs[z] * cc + ty[z, own, :] * cn + ty[z, HALO - 1:HALO + ny - 1, :] * cs
             + txp[z] * ce + txm[z] * cw)
        for r in range(3):
            out[r, z] = w[r, z] + qv[r, z] * g
        return 0

    step = nz // parts
    outs = [corr]
    for part in range(parts):
        lax.fori_loop(part * step, (part + 1) * step, finish, 0)
        chunk = slice(part * step, (part + 1) * step)
        outs.append(pltpu.make_async_copy(out.at[:, chunk], new_hbm.at[:, chunk], out_sem.at[part]))
        outs[-1].start()
    for copy in outs:
        copy.wait()


def per_device(sizes, state, right_side, permeability, pore_volume, facies, storage_table, coupling_table):
    _, nz, ny, nx = state.shape
    sizes = sizes + (nz, ny, nx)
    f32 = jnp.float32
    ngz = sizes[2]
    cells = (nz, ny, nx)
    vmem = lambda *shape: pltpu.VMEM(shape, f32)
    hbm = pl.BlockSpec(memory_space=pltpu.HBM)
    dma = lambda n: pltpu.SemaphoreType.DMA((n,))
    ey = ny + 2 * HALO
    groups, per, xtiles = column_plan(nz, ny, nx)
    strips = len(strip_plan(ny, nx))
    facets = storage_table.shape[0]
    in_vmem = pl.BlockSpec(memory_space=pltpu.VMEM)
    handed = 4 * nx * (9 * nz * ny + nz * ey + 3 * ey)
    limit = 16384 * ((VMEM_BYTES - handed) // 16384)
    middle = pl.pallas_call(
        functools.partial(kernel, sizes),
        out_shape=(vmem(3, *cells), vmem(3, *cells), vmem(*cells), vmem(nz, ey, nx), vmem(*cells), vmem(*cells),
                   vmem(3, ey, nx)),
        in_specs=[hbm, hbm, hbm, hbm, hbm, hbm, hbm],
        out_specs=(in_vmem,) * 7,
        scratch_shapes=[
            vmem(4, nz + 2, ey, nx), vmem(nz, ey, nx), vmem(3, *cells),
            pltpu.VMEM(cells, permeability.dtype), pltpu.VMEM(cells, pore_volume.dtype),
            vmem(2, 2, 2 * nz, nx), vmem(2, 2, 2 * nz, nx),
            vmem(2, 2, xtiles, HALO, nx), vmem(2, 2, 2, xtiles, HALO, nx), vmem(4, xtiles, HALO, nx),
            vmem(3, nz, nx), vmem(nz + 1, ny, nx), vmem(2, ey, nx),
            vmem(ngz, PLANES, ny, nx), vmem(strips, HALO, nx),
            vmem(2, ngz, PLANES, HALO, nx), vmem(2, ngz, strips, HALO, nx), vmem(4, ngz, HALO, nx),
            vmem(2, ey + 2 * HALO, nx),
            pltpu.SMEM((nz,), facies.dtype), pltpu.SMEM((3, facets, 3), f32), pltpu.SMEM((3, facets, 3), f32),
            pltpu.SMEM((NCOEF, facets), f32),
            pltpu.SemaphoreType.REGULAR, pltpu.SemaphoreType.REGULAR, dma(7), dma(6), dma(6), dma(4), dma(4),
        ],
        compiler_params=pltpu.CompilerParams(collective_id=0, has_side_effects=True, vmem_limit_bytes=limit),
        name="cpr_apply",
    )(facies, storage_table.transpose(1, 0, 2), coupling_table.transpose(1, 0, 2),
      state, right_side, permeability, pore_volume)
    parts = 8 if nz % 8 == 0 else 1
    return tuple(pl.pallas_call(
        functools.partial(finish_kernel, parts),
        out_shape=(jax.ShapeDtypeStruct(state.shape, f32), jax.ShapeDtypeStruct((ny, nx), f32)),
        in_specs=[in_vmem] * 7,
        out_specs=(hbm, hbm),
        scratch_shapes=[vmem(3, *cells), dma(parts + 1)],
        compiler_params=pltpu.CompilerParams(vmem_limit_bytes=16 * 2**20),
        name="cpr_finish",
    )(*middle))


def solution(mesh):
    sizes = (mesh.shape["gx"], mesh.shape["gy"], mesh.shape["gz"])
    return jax.shard_map(
        functools.partial(per_device, sizes),
        mesh=mesh,
        in_specs=(
            P(None, "gz", "gy", "gx"),
            P(None, "gz", "gy", "gx"),
            P("gz", "gy", "gx"),
            P("gz", "gy", "gx"),
            P("gz"),
            P(),
            P(),
        ),
        out_specs=(P(None, "gz", "gy", "gx"), P("gy", "gx")),
        check_vma=False,
    )
```

profile of v0, /device:TPU:0, one launch (start us, length us, event | category | flops | bytes accessed | tf_op | source)
XLA Modules:
  0.0 13.5 jit_solution(109932561646916360)
XLA Ops:
  0.6 11.8 %cpr_apply.1 = (f32[3,16,40,128]{3,2,1,0:T(8,128)S(1)}, f32[3,16,40,128]{3,2,1,0:T(8,128)S(1)}, f32[16,40,128]{2,1,0:T(8,128)S(1)}, f32[16,56,128]{2,1,0:T(8,128...) custom-call(s32[16]{0:T(128)} %facies_hbm.1, f32[3,4,3]{2,1,0:T(4,128)} %bitcast.2, ...), custom_call_target="tpu_custom_call" | custom-call | tf_op jit(solution)/shard_map/cpr_apply/pallas_call | solution.py:620
  12.5 1.0 %cpr_finish.1 = (f32[3,16,40,128]{3,2,1,0:T(8,128)}, f32[40,128]{1,0:T(8,128)}) custom-call(f32[3,16,40,128]{3,2,1,0:T(8,128)S(1)} %get-tuple-element.9.w, f32[3,16,40,128]{3,2,1,0:T(8,128)S(1)} %get-tuple-element.10.qv, f32[16,40,128]{2,1,0:T(8,128)S(1)} %get-tuple-element.11.tzs, f32[16,56,128]{2,1,0:T(8,128)S(1)} %get-tuple-element.12.ty, ...), custom_call_target="tpu_custom_call" | custom-call | tf_op jit(solution)/shard_map/cpr_finish/pallas_call | solution.py:644
where the time goes:
time: 13.7 us; the launch traced here: 13.5 us
  Pallas kernels  12.9 us (94%)
  between operations  0.64 us (5%)
    pallas_call x1, Pallas kernels, per_device(): pl.pallas_call(functools.partial(kernel, sizes), out_shape=(vmem(3, *cell...  11.8 us
    pallas_call x1, Pallas kernels, per_device(): pl.pallas_call(functools.partial(finish_kernel, parts), out_shape=(jax.Sh...  1.05 us

commit v1 on v0

--- a/solution.py
+++ b/solution.py
@@ -55,7 +55,7 @@
 def kernel(sizes, facies_hbm, mtab_hbm, ktab_hbm, state_hbm, rhs_hbm, perm_hbm, pore_hbm,
            w, qv, tzs, ty, txp, txm, final,
            u, pcb, rhs, permb, poreb, ysend, yrecv, xsend, xrecv, edge, rowk, tzf, shifted,
-           zplanes, strips, cyrecv, cxrecv, cdrecv, field,
+           zplanes, ystrips, strips, cyrecv, cxrecv, cdrecv, vsend, vrecv, lsend, lrecv, field,
            facies, mtab, ktab, ctab, near_sem, far_sem, in_sem, h_send, h_recv, c_send, c_recv):
     ngx, ngy, ngz, nz, ny, nx = sizes
     ix, iy, iz = lax.axis_index("gx"), lax.axis_index("gy"), lax.axis_index("gz")
@@ -76,7 +76,7 @@
         return {"gx": ix + dx, "gy": iy + dy, "gz": iz}
 
     barrier = pltpu.get_barrier_semaphore()
-    for side in SIDES[:4]:
+    for side in (SIDES[2], SIDES[3], SIDES[0], SIDES[1]):
         @pl.when(exists(*side))
         def _(side=side):
             pl.semaphore_signal(barrier, inc=1, device_id=at(*side), device_id_type=MESH)
@@ -106,10 +106,10 @@
     for cond, refs in (
         (iz == 0, [u.at[:, 0, own]]),
         (iz == ngz - 1, [u.at[:, nz + 1, own]]),
-        (iy == 0, [yrecv.at[:, 0], cyrecv.at[0]]),
-        (iy == ngy - 1, [yrecv.at[:, 1], cyrecv.at[1]]),
-        (ix == 0, [xrecv.at[:, 0], cxrecv.at[0]]),
-        (ix == ngx - 1, [xrecv.at[:, 1], cxrecv.at[1]]),
+        (iy == 0, [yrecv.at[:, 0], cyrecv.at[0], lrecv.at[0]]),
+        (iy == ngy - 1, [yrecv.at[:, 1], cyrecv.at[1], lrecv.at[1]]),
+        (ix == 0, [xrecv.at[:, 0], cxrecv.at[0], vrecv.at[0]]),
+        (ix == ngx - 1, [xrecv.at[:, 1], cxrecv.at[1], vrecv.at[1]]),
         (jnp.logical_or(iy == 0, ix == 0), [cdrecv.at[0]]),
         (jnp.logical_or(iy == 0, ix == ngx - 1), [cdrecv.at[1]]),
         (jnp.logical_or(iy == ngy - 1, ix == 0), [cdrecv.at[2]]),
@@ -137,6 +137,110 @@
     first8, last8 = lane8 == 0, lane8 == nx - 1
     nil8 = jnp.zeros((HALO, nx), f32)
 
+    def packed_columns(values):
+        out = [nil8] * xtiles
+        for z, g, x in values:
+            place = (g % per) * nz + z
+            out[g // per] = jnp.where(pair8 == place, pltpu.roll(x, 2 * place + 1, 1), out[g // per])
+        return out
+
+    def swapped(x):
+        return jnp.where(even8, pltpu.roll(x, nx - 1, 1), pltpu.roll(x, 1, 1))
+
+    loads[0].wait()
+    values = []
+    for z in range(nz):
+        r = 0.5 / permb[z].astype(f32)
+        u[3, z + 1, own, :] = r
+        for side, at_row in ((0, 0), (1, ny - 1)):
+            ysend[0, side, nz + z:nz + z + 1, :] = r[at_row:at_row + 1]
+        values += [(z, g, r[g * HALO:(g + 1) * HALO]) for g in range(groups)]
+    packed = packed_columns(values)
+    for t in range(xtiles):
+        xsend[0, 1, t] = packed[t]
+
+    loads[1].wait()
+    values = []
+    for z in range(nz):
+        k0 = [coefficient(ktab, z, 0, k) for k in range(3)]
+        pc = k0[0] * u[0, z + 1, own, :] + k0[1] * u[1, z + 1, own, :] + k0[2] * u[2, z + 1, own, :]
+        pcb[z, own, :] = pc
+        for side, at_row in ((0, 0), (1, ny - 1)):
+            ysend[0, side, z:z + 1, :] = pc[at_row:at_row + 1]
+        values += [(z, g, pc[g * HALO:(g + 1) * HALO]) for g in range(groups)]
+    packed = packed_columns(values)
+    for t in range(xtiles):
+        xsend[0, 0, t] = packed[t]
+
+    beside_y = exists(-1, 0).astype(jnp.int32) + exists(1, 0).astype(jnp.int32)
+    beside_x = exists(0, -1).astype(jnp.int32) + exists(0, 1).astype(jnp.int32)
+    pl.semaphore_wait(barrier, beside_y + beside_x + (ngz - 1))
+
+    def remote(src, dst, send, recv, device):
+        return pltpu.make_async_remote_copy(src_ref=src, dst_ref=dst, send_sem=send, recv_sem=recv,
+                                            device_id=device, device_id_type=MESH)
+
+    def start(copies):
+        for sends, copy in copies:
+            @pl.when(sends)
+            def _(copy=copy):
+                copy.start()
+
+    def y_copies(batch):
+        s = h_send.at[2 + batch], h_recv.at[2 + batch]
+        return [(exists(1, 0), remote(ysend.at[batch, 1], yrecv.at[batch, 0], *s, at(1, 0))),
+                (exists(-1, 0), remote(ysend.at[batch, 0], yrecv.at[batch, 1], *s, at(-1, 0)))]
+
+    def x_copies(batch):
+        s = h_send.at[4 + batch], h_recv.at[4 + batch]
+        return [(exists(0, 1), remote(xsend.at[batch], xrecv.at[batch, 0], *s, at(0, 1))),
+                (exists(0, -1), remote(xsend.at[batch], xrecv.at[batch, 1], *s, at(0, -1)))]
+
+    def z_device(d):
+        return {"gx": ix, "gy": iy, "gz": iz + d}
+
+    z_up = remote(u.at[:, nz, own], u.at[:, 0, own], h_send.at[0], h_recv.at[0], z_device(1))
+    z_down = remote(u.at[:, 1, own], u.at[:, nz + 1, own], h_send.at[1], h_recv.at[1], z_device(-1))
+    has_below, has_above = iz > 0, iz < ngz - 1
+
+    start(y_copies(0))
+    start(x_copies(0))
+    start([(has_above, z_up), (has_below, z_down)])
+    for side in SIDES[:4]:
+        @pl.when(exists(*side))
+        def _(side=side):
+            pl.semaphore_signal(near_sem, inc=1, device_id=at(*side), device_id_type=MESH)
+    signal_peers(near_sem)
+
+    def counted(count, cases, descriptor, done):
+        for n, ref in cases:
+            @pl.when(count == n)
+            def _(ref=ref):
+                done(descriptor(ref))
+
+    def wait_many(count, cases, send, recv, sent):
+        counted(count, cases, lambda ref: remote(ref, ref, send, recv, z_device(0)),
+                (lambda c: c.wait_send()) if sent else (lambda c: c.wait_recv()))
+
+    def wait_y(batch, sent):
+        wait_many(beside_y, ((1, yrecv.at[batch, 0]), (2, yrecv.at[batch])), h_send.at[2 + batch], h_recv.at[2 + batch], sent)
+
+    def wait_x(batch, sent):
+        wait_many(beside_x, ((1, xrecv.at[batch, 0]), (2, xrecv.at[batch])), h_send.at[4 + batch], h_recv.at[4 + batch], sent)
+
+    for i in range(2):
+        values = []
+        for z in range(nz):
+            c = u[1 + i, z + 1, own, :]
+            for side, at_row in ((0, 0), (1, ny - 1)):
+                ysend[1, side, i * nz + z:i * nz + z + 1, :] = c[at_row:at_row + 1]
+            values += [(z, g, c[g * HALO:(g + 1) * HALO]) for g in range(groups)]
+        packed = packed_columns(values)
+        for t in range(xtiles):
+            xsend[1, i, t] = packed[t]
+    start(x_copies(1))
+    start(y_copies(1))
+
     for f in range(ktab.shape[1]):
         values = block_scalars([[mtab[r, f, c] for c in range(3)] for r in range(3)],
                                [[ktab[r, f, c] for c in range(3)] for r in range(3)])
@@ -149,110 +253,6 @@
             value = coefficient(ktab, z, 0, k)
             rowk[k, z:z + 1, :] = jnp.full((1, nx), value, f32)
             lanek[k] = jnp.where(layer_of_lane == z, value, lanek[k])
-
-    def packed_columns(values):
-        out = [nil8] * xtiles
-        for z, g, x in values:
-            place = (g % per) * nz + z
-            out[g // per] = jnp.where(pair8 == place, pltpu.roll(x, 2 * place + 1, 1), out[g // per])
-        return out
-
-    def swapped(x):
-        return jnp.where(even8, pltpu.roll(x, nx - 1, 1), pltpu.roll(x, 1, 1))
-
-    loads[0].wait()
-    values = []
-    for z in range(nz):
-        r = 0.5 / permb[z].astype(f32)
-        u[3, z + 1, own, :] = r
-        for side, at_row in ((0, 0), (1, ny - 1)):
-            ysend[0, side, nz + z:nz + z + 1, :] = r[at_row:at_row + 1]
-        values += [(z, g, r[g * HALO:(g + 1) * HALO]) for g in range(groups)]
-    packed = packed_columns(values)
-    for t in range(xtiles):
-        xsend[0, 1, t] = packed[t]
-
-    loads[1].wait()
-    values = []
-    for z in range(nz):
-        k0 = [coefficient(ktab, z, 0, k) for k in range(3)]
-        pc = k0[0] * u[0, z + 1, own, :] + k0[1] * u[1, z + 1, own, :] + k0[2] * u[2, z + 1, own, :]
-        pcb[z, own, :] = pc
-        for side, at_row in ((0, 0), (1, ny - 1)):
-            ysend[0, side, z:z + 1, :] = pc[at_row:at_row + 1]
-        values += [(z, g, pc[g * HALO:(g + 1) * HALO]) for g in range(groups)]
-    packed = packed_columns(values)
-    for t in range(xtiles):
-        xsend[0, 0, t] = packed[t]
-
-    beside_y = exists(-1, 0).astype(jnp.int32) + exists(1, 0).astype(jnp.int32)
-    beside_x = exists(0, -1).astype(jnp.int32) + exists(0, 1).astype(jnp.int32)
-    pl.semaphore_wait(barrier, beside_y + beside_x + (ngz - 1))
-
-    def remote(src, dst, send, recv, device):
-        return pltpu.make_async_remote_copy(src_ref=src, dst_ref=dst, send_sem=send, recv_sem=recv,
-                                            device_id=device, device_id_type=MESH)
-
-    def start(copies):
-        for sends, copy in copies:
-            @pl.when(sends)
-            def _(copy=copy):
-                copy.start()
-
-    def y_copies(batch):
-        s = h_send.at[2 + batch], h_recv.at[2 + batch]
-        return [(exists(1, 0), remote(ysend.at[batch, 1], yrecv.at[batch, 0], *s, at(1, 0))),
-                (exists(-1, 0), remote(ysend.at[batch, 0], yrecv.at[batch, 1], *s, at(-1, 0)))]
-
-    def x_copies(batch):
-        s = h_send.at[4 + batch], h_recv.at[4 + batch]
-        return [(exists(0, 1), remote(xsend.at[batch], xrecv.at[batch, 0], *s, at(0, 1))),
-                (exists(0, -1), remote(xsend.at[batch], xrecv.at[batch, 1], *s, at(0, -1)))]
-
-    def z_device(d):
-        return {"gx": ix, "gy": iy, "gz": iz + d}
-
-    z_up = remote(u.at[:, nz, own], u.at[:, 0, own], h_send.at[0], h_recv.at[0], z_device(1))
-    z_down = remote(u.at[:, 1, own], u.at[:, nz + 1, own], h_send.at[1], h_recv.at[1], z_device(-1))
-    has_below, has_above = iz > 0, iz < ngz - 1
-
-    start(x_copies(0))
-    start(y_copies(0))
-    start([(has_above, z_up), (has_below, z_down)])
-    for side in SIDES[:4]:
-        @pl.when(exists(*side))
-        def _(side=side):
-            pl.semaphore_signal(near_sem, inc=1, device_id=at(*side), device_id_type=MESH)
-    signal_peers(near_sem)
-
-    def counted(count, cases, descriptor, done):
-        for n, ref in cases:
-            @pl.when(count == n)
-            def _(ref=ref):
-                done(descriptor(ref))
-
-    def wait_many(count, cases, send, recv, sent):
-        counted(count, cases, lambda ref: remote(ref, ref, send, recv, z_device(0)),
-                (lambda c: c.wait_send()) if sent else (lambda c: c.wait_recv()))
-
-    def wait_y(batch, sent):
-        wait_many(beside_y, ((1, yrecv.at[batch, 0]), (2, yrecv.at[batch])), h_send.at[2 + batch], h_recv.at[2 + batch], sent)
-
-    def wait_x(batch, sent):
-        wait_many(beside_x, ((1, xrecv.at[batch, 0]), (2, xrecv.at[batch])), h_send.at[4 + batch], h_recv.at[4 + batch], sent)
-
-    for i in range(2):
-        values = []
-        for z in range(nz):
-            c = u[1 + i, z + 1, own, :]
-            for side, at_row in ((0, 0), (1, ny - 1)):
-                ysend[1, side, i * nz + z:i * nz + z + 1, :] = c[at_row:at_row + 1]
-            values += [(z, g, c[g * HALO:(g + 1) * HALO]) for g in range(groups)]
-        packed = packed_columns(values)
-        for t in range(xtiles):
-            xsend[1, i, t] = packed[t]
-    start(x_copies(1))
-    start(y_copies(1))
 
     loads[2].wait()
     loads[3].wait()
@@ -334,30 +334,57 @@
     pl.semaphore_wait(near_sem, beside_y + beside_x + (ngz - 1))
     signal_peers(far_sem)
 
+    planes = [p_rhs, p_dia, s_ty, s_tx]
+    group8 = lax.shift_right_logical(lane8, 4)
+    last_head = len(packing[:2]) - 1
+    for p in range(PLANES):
+        ystrips[0, p] = planes[p][0]
+        ystrips[1, p] = planes[p][groups - 1]
+    for i, tiles in enumerate(packing):
+        strip = nil8
+        for j, g in enumerate(tiles):
+            for p in range(PLANES):
+                slot = j * PLANES + p
+                strip = jnp.where(group8 == slot, pltpu.roll(planes[p][g], (2 * HALO * slot + HALO) % nx, 1), strip)
+        strips[i] = strip
+
+    pl.semaphore_wait(far_sem, ngz - 1)
+
+    def to_all(dy, dx, src, dst, sem):
+        return [(exists(dy, dx), remote(src, dst, c_send.at[sem], c_recv.at[sem],
+                                        {"gx": ix + dx, "gy": iy + dy, "gz": lax.rem(iz + d, ngz)})) for d in range(ngz)]
+
+    for dy, dx in SIDES[4:]:
+        start(to_all(dy, dx, strips.at[0 if dy < 0 else last_head], cdrecv.at[(1 - dy) + (1 - dx) // 2, iz], 3))
+    for dx in (-1, 1):
+        start(to_all(0, dx, strips, cxrecv.at[(1 - dx) // 2, iz], 2))
+    for dy in (-1, 1):
+        start(to_all(dy, 0, ystrips.at[(1 + dy) // 2], cyrecv.at[(1 - dy) // 2, iz], 1))
+
     wait_y(0, False)
-    for side, at_row, g in ((0, 0, 0), (1, HALO - 1, groups - 1)):
+    top8, bottom8 = row8 == 0, row8 == HALO - 1
+    lines = nil8
+    for side, g, here, beyond in ((0, 0, top8, bottom8), (1, groups - 1, bottom8, top8)):
         there = yrecv[0, side, nz:, :]
         t = jnp.where(there > 0.0, 1.0 / (ysend[0, side, nz:, :] + there), 0.0)
+        moved = jnp.sum(t * (ysend[0, side, :nz, :] - yrecv[0, side, :nz, :]), axis=0, keepdims=True)
+        weight = jnp.sum(rowk[0] * t, axis=0, keepdims=True)
+        changes = [jnp.where(here, -moved, jnp.where(beyond, moved, 0.0)),
+                   jnp.where(jnp.logical_or(here, beyond), weight, 0.0),
+                   jnp.where(bottom8, weight, 0.0)]
+        packed = nil8
+        for p in range(3):
+            packed = jnp.where(group8 == p, pltpu.roll(changes[p], 2 * HALO * p + HALO, 1), packed)
+        vsend[side] = packed
         for z in range(nz):
             edge_row = HALO - 1 + side * ny
             ty[z, edge_row:edge_row + 1, :] = t[z:z + 1]
-        moved = jnp.sum(t * (ysend[0, side, :nz, :] - yrecv[0, side, :nz, :]), axis=0, keepdims=True)
-        weight = jnp.sum(rowk[0] * t, axis=0, keepdims=True)
-        here = row8 == at_row
-        p_rhs[g] = p_rhs[g] - jnp.where(here, moved, 0.0)
-        p_dia[g] = p_dia[g] + jnp.where(here, weight, 0.0)
-        if side:
-            s_ty[g] = s_ty[g] + jnp.where(here, weight, 0.0)
-    planes = [p_rhs, p_dia, s_ty, s_tx]
-    group8 = lax.shift_right_logical(lane8, 4)
-    packed = []
-    for tiles in packing:
-        strip = nil8
-        for i, g in enumerate(tiles):
-            for p in range(PLANES):
-                slot = i * PLANES + p
-                strip = jnp.where(group8 == slot, pltpu.roll(planes[p][g], (2 * HALO * slot + HALO) % nx, 1), strip)
-        packed.append(strip)
+        for p in range(3 if side else 2):
+            planes[p][g] = planes[p][g] + jnp.where(here, changes[p], 0.0)
+        lines = jnp.where(row8 == 2 * side, moved, jnp.where(row8 == 2 * side + 1, weight, lines))
+    zplanes[iz, PLANES * groups] = lines
+    for dx in (-1, 1):
+        start(to_all(0, dx, vsend, vrecv.at[(1 - dx) // 2, iz], 4))
 
     wait_x(0, False)
     flux, weights, faces, outside = [], [], [], []
@@ -370,6 +397,7 @@
         outside.append(there[0])
     in16 = lax.rem(lane8, 2 * HALO)
     for i, tiles in enumerate(packing):
+        across = nil8
         for j, g in enumerate(tiles):
             low = (g % per) * 2 * nz
             block = jnp.logical_and(lane8 >= low, lane8 < low + 2 * nz)
@@ -378,40 +406,28 @@
                 for parity in (even8, jnp.logical_not(even8)):
                     chosen = jnp.where(jnp.logical_and(block, parity), values[g // per], 0.0)
                     sums.append(jnp.sum(chosen, axis=1, keepdims=True))
-            for p, left, right, sign in ((0, sums[0], sums[1], -1.0), (1, sums[2], sums[3], 1.0), (3, None, sums[3], 1.0)):
+            flux_l, flux_r, weight_l, weight_r = sums
+            changes = [jnp.where(first8, -flux_l, jnp.where(last8, -flux_r, 0.0)),
+                       jnp.where(first8, weight_l, jnp.where(last8, weight_r, 0.0)),
+                       jnp.where(last8, weight_r, 0.0)]
+            for p, change in zip((0, 1, 3), changes):
+                planes[p][g] = planes[p][g] + change
+            for p, left, right in ((0, flux_l, flux_r), (1, weight_l, weight_r), (3, weight_l, 0.0)):
                 slot = (j * PLANES + p) * 2 * HALO
-                at_left, at_right = lane8 == slot + HALO, lane8 == slot + HALO - 1
-                change = jnp.where(last8, sign * right, 0.0)
-                moved = jnp.where(at_right, sign * right, 0.0)
-                if left is not None:
-                    change = jnp.where(first8, sign * left, change)
-                    moved = jnp.where(at_left, sign * left, moved)
-                planes[p][g] = planes[p][g] + change
-                packed[i] = packed[i] + moved
-    for i in range(len(packing)):
-        strips[i] = packed[i]
+                across = jnp.where(lane8 == slot + HALO - 1, left, jnp.where(lane8 == slot + HALO, right, across))
+            for side, head in ((0, 0), (1, groups - 1)):
+                if g == head:
+                    for n in range(3):
+                        lsend[side, n] = changes[n]
+        zplanes[iz, PLANES * groups + 1 + i] = across
+        for side, head in ((0, 0), (1, last_head)):
+            if i == head:
+                lsend[side, 3] = across
+    for dy in (-1, 1):
+        start(to_all(dy, 0, lsend.at[(1 + dy) // 2], lrecv.at[(1 - dy) // 2, iz], 5))
     for p in range(PLANES):
         for g in range(groups):
-            zplanes[iz, p, tile_of(g), :] = planes[p][g]
-
-    pl.semaphore_wait(far_sem, ngz - 1)
-    copies = []
-    for n, (dy, dx) in enumerate(SIDES[4:]):
-        into = (1 - dy) + (1 - dx) // 2
-        src = strips.at[0 if dy < 0 or len(packing) == 1 else 1]
-        for d in range(ngz):
-            device = {"gx": ix + dx, "gy": iy + dy, "gz": lax.rem(iz + d, ngz)}
-            copies.append((exists(dy, dx), remote(src, cdrecv.at[into, iz], c_send.at[3], c_recv.at[3], device)))
-    for dx in (-1, 1):
-        for d in range(ngz):
-            device = {"gx": ix + dx, "gy": iy, "gz": lax.rem(iz + d, ngz)}
-            copies.append((exists(0, dx), remote(strips, cxrecv.at[(1 - dx) // 2, iz], c_send.at[2], c_recv.at[2], device)))
-    for dy in (-1, 1):
-        src = zplanes.at[iz, :, 0:HALO] if dy < 0 else zplanes.at[iz, :, ny - HALO:ny]
-        for d in range(ngz):
-            device = {"gx": ix, "gy": iy + dy, "gz": lax.rem(iz + d, ngz)}
-            copies.append((exists(dy, 0), remote(src, cyrecv.at[(1 - dy) // 2, iz], c_send.at[1], c_recv.at[1], device)))
-    start(copies)
+            zplanes[iz, p * groups + g] = planes[p][g]
     for d in range(1, ngz):
         remote(zplanes.at[iz], zplanes.at[iz], c_send.at[0], c_recv.at[0],
                {"gx": ix, "gy": iy, "gz": lax.rem(iz + d, ngz)}).start()
@@ -492,19 +508,41 @@
     wait_many(beside_y, y_cases, c_send.at[1], c_recv.at[1], False)
     wait_many(beside_x, x_cases, c_send.at[2], c_recv.at[2], False)
     wait_many(corners, d_cases, c_send.at[3], c_recv.at[3], False)
-
-    def gathered(ref, *index):
-        total = ref[index[0], 0] if not index[1:] else ref[(index[0], 0) + index[1:]]
+    v_cases = ((1, vrecv.at[0]), (2, vrecv))
+    l_cases = ((1, lrecv.at[0]), (2, lrecv))
+    wait_many(beside_x, v_cases, c_send.at[4], c_recv.at[4], False)
+    wait_many(beside_y, l_cases, c_send.at[5], c_recv.at[5], False)
+
+    def gathered(part):
+        total = part(0)
         for i in range(1, ngz):
-            total = total + (ref[index[0], i] if not index[1:] else ref[(index[0], i) + index[1:]])
+            total = total + part(i)
         return total
 
     rows = ny + 2 * HALO
     elane = lax.broadcasted_iota(jnp.int32, (rows, nx), 1)
     efirst, elast = elane == 0, elane == nx - 1
     left_part = in16 < HALO
-    side_tiles = [jnp.where(left_part, gathered(cxrecv, 0, i), gathered(cxrecv, 1, i)) for i in range(len(packing))]
-    corner_tiles = [jnp.where(left_part, gathered(cdrecv, 2 * v), gathered(cdrecv, 2 * v + 1)) for v in range(2)]
+    lines = gathered(lambda i: zplanes[i, PLANES * groups])
+    late = [jnp.where(left_part, gathered(lambda i: vrecv[0, i, v]), gathered(lambda i: vrecv[1, i, v])) for v in range(2)]
+    beside = [[gathered(lambda i: lrecv[side, i, n]) for n in range(4)] for side in range(2)]
+    side_tiles = [jnp.where(left_part, gathered(lambda i: cxrecv[0, i, t]), gathered(lambda i: cxrecv[1, i, t]))
+                  + gathered(lambda i: zplanes[i, PLANES * groups + 1 + t]) for t in range(len(packing))]
+    side_tiles[0] = side_tiles[0] + jnp.where(top8, late[0], 0.0)
+    side_tiles[last_head] = side_tiles[last_head] + jnp.where(bottom8, late[1], 0.0)
+    corner_tiles = [jnp.where(left_part, gathered(lambda i: cdrecv[2 * v, i]), gathered(lambda i: cdrecv[2 * v + 1, i]))
+                    + jnp.where(bottom8 if v == 0 else top8, late[v], 0.0) + beside[v][3] for v in range(2)]
+    end_tiles = []
+    for side, here in ((0, bottom8), (1, top8)):
+        moved, weight = lines[2 * side:2 * side + 1], lines[2 * side + 1:2 * side + 2]
+        tiles = [gathered(lambda i: cyrecv[side, i, p]) for p in range(PLANES)]
+        for n, p in enumerate((0, 1, 3)):
+            tiles[p] = tiles[p] + beside[side][n]
+        tiles[0] = tiles[0] + jnp.where(here, moved, 0.0)
+        tiles[1] = tiles[1] + jnp.where(here, weight, 0.0)
+        if side == 0:
+            tiles[2] = tiles[2] + jnp.where(here, weight, 0.0)
+        end_tiles.append(tiles)
     where_is = {g: (i, j) for i, tiles in enumerate(packing) for j, g in enumerate(tiles)}
     strip8 = jnp.logical_or(lane8 < HALO, lane8 >= nx - HALO)
 
@@ -517,12 +555,8 @@
         return jnp.where(strip8, pltpu.roll(tile, (2 * nx - 2 * HALO * slot - HALO) % nx, 1), 0.0)
 
     b = [jnp.concatenate([border_of(p, g) for g in range(-1, groups + 1)], axis=0) for p in range(PLANES)]
-    a = []
-    for p in range(PLANES):
-        plane = zplanes[0, p]
-        for i in range(1, ngz):
-            plane = plane + zplanes[i, p]
-        a.append(jnp.concatenate([gathered(cyrecv, 0, p), plane, gathered(cyrecv, 1, p)], axis=0))
+    a = [jnp.concatenate([end_tiles[0][p]] + [gathered(lambda i: zplanes[i, p * groups + g]) for g in range(groups)]
+                         + [end_tiles[1][p]], axis=0) for p in range(PLANES)]
 
     def east(a, b):
         ra, rb = pltpu.roll(a, nx - 1, 1), pltpu.roll(b, nx - 1, 1)
@@ -573,6 +607,8 @@
     wait_many(beside_y, y_cases, c_send.at[1], c_recv.at[1], True)
     wait_many(beside_x, x_cases, c_send.at[2], c_recv.at[2], True)
     wait_many(corners, d_cases, c_send.at[3], c_recv.at[3], True)
+    wait_many(beside_x, v_cases, c_send.at[4], c_recv.at[4], True)
+    wait_many(beside_y, l_cases, c_send.at[5], c_recv.at[5], True)
 
 
 def finish_kernel(parts, w, qv, tzs, ty, txp, txm, final, new_hbm, corr_hbm, out, out_sem):
@@ -629,12 +665,13 @@
             vmem(2, 2, 2 * nz, nx), vmem(2, 2, 2 * nz, nx),
             vmem(2, 2, xtiles, HALO, nx), vmem(2, 2, 2, xtiles, HALO, nx), vmem(4, xtiles, HALO, nx),
             vmem(3, nz, nx), vmem(nz + 1, ny, nx), vmem(2, ey, nx),
-            vmem(ngz, PLANES, ny, nx), vmem(strips, HALO, nx),
+            vmem(ngz, PLANES * groups + 1 + strips, HALO, nx), vmem(2, PLANES, HALO, nx), vmem(strips, HALO, nx),
             vmem(2, ngz, PLANES, HALO, nx), vmem(2, ngz, strips, HALO, nx), vmem(4, ngz, HALO, nx),
+            vmem(2, HALO, nx), vmem(2, ngz, 2, HALO, nx), vmem(2, 4, HALO, nx), vmem(2, ngz, 4, HALO, nx),
             vmem(2, ey + 2 * HALO, nx),
             pltpu.SMEM((nz,), facies.dtype), pltpu.SMEM((3, facets, 3), f32), pltpu.SMEM((3, facets, 3), f32),
             pltpu.SMEM((NCOEF, facets), f32),
-            pltpu.SemaphoreType.REGULAR, pltpu.SemaphoreType.REGULAR, dma(7), dma(6), dma(6), dma(4), dma(4),
+            pltpu.SemaphoreType.REGULAR, pltpu.SemaphoreType.REGULAR, dma(7), dma(6), dma(6), dma(6), dma(6),
         ],
         compiler_params=pltpu.CompilerParams(collective_id=0, has_side_effects=True, vmem_limit_bytes=limit),
         name="cpr_apply",

time: 13.7 us -> 12.9 us (0.942)
  Pallas kernels: 12.9 us -> 12.1 us
    pallas_call x1, Pallas kernels: 11.8 us -> 11 us  [per_device(): pl.pallas_call(functools.partial(kernel, sizes), out_shape=(vmem(3, *cell...]
where the time goes in v1:
time: 12.9 us; the launch traced here: 12.7 us
  Pallas kernels  12.1 us (94%)
  between operations  0.64 us (5%)
    pallas_call x1, Pallas kernels, per_device(): pl.pallas_call(functools.partial(kernel, sizes), out_shape=(vmem(3, *cell...  11 us
    pallas_call x1, Pallas kernels, per_device(): pl.pallas_call(functools.partial(finish_kernel, parts), out_shape=(jax.Sh...  1.05 us

profile of v1, /device:TPU:0, one launch (start us, length us, event | category | flops | bytes accessed | tf_op | source)
XLA Modules:
  0.0 12.7 jit_solution(15931512391179836397)
XLA Ops:
  0.6 11.0 %cpr_apply.1 = (f32[3,16,40,128]{3,2,1,0:T(8,128)S(1)}, f32[3,16,40,128]{3,2,1,0:T(8,128)S(1)}, f32[16,40,128]{2,1,0:T(8,128)S(1)}, f32[16,56,128]{2,1,0:T(8,128...) custom-call(s32[16]{0:T(128)} %facies_hbm.1, f32[3,4,3]{2,1,0:T(4,128)} %bitcast.2, ...), custom_call_target="tpu_custom_call" | custom-call | tf_op jit(solution)/shard_map/cpr_apply/pallas_call | solution.py:656
  11.7 1.0 %cpr_finish.1 = (f32[3,16,40,128]{3,2,1,0:T(8,128)}, f32[40,128]{1,0:T(8,128)}) custom-call(f32[3,16,40,128]{3,2,1,0:T(8,128)S(1)} %get-tuple-element.9.w, f32[3,16,40,128]{3,2,1,0:T(8,128)S(1)} %get-tuple-element.10.qv, f32[16,40,128]{2,1,0:T(8,128)S(1)} %get-tuple-element.11.tzs, f32[16,56,128]{2,1,0:T(8,128)S(1)} %get-tuple-element.12.ty, ...), custom_call_target="tpu_custom_call" | custom-call | tf_op jit(solution)/shard_map/cpr_finish/pallas_call | solution.py:681

commit v2 on v1

--- a/solution.py
+++ b/solution.py
@@ -55,14 +55,15 @@
 def kernel(sizes, facies_hbm, mtab_hbm, ktab_hbm, state_hbm, rhs_hbm, perm_hbm, pore_hbm,
            w, qv, tzs, ty, txp, txm, final,
            u, pcb, rhs, permb, poreb, ysend, yrecv, xsend, xrecv, edge, rowk, tzf, shifted,
-           zplanes, ystrips, strips, cyrecv, cxrecv, cdrecv, vsend, vrecv, lsend, lrecv, field,
-           facies, mtab, ktab, ctab, near_sem, far_sem, in_sem, h_send, h_recv, c_send, c_recv):
+           zplanes, ystrips, strips, cyrecv, cxrecv, cdrecv, vsend, lsend, field,
+           facies, mtab, ktab, ctab, near_sem, far_sem, in_sem, h_recv, c_recv):
     ngx, ngy, ngz, nz, ny, nx = sizes
     ix, iy, iz = lax.axis_index("gx"), lax.axis_index("gy"), lax.axis_index("gz")
     own = slice(HALO, HALO + ny)
     groups, per, xtiles = column_plan(nz, ny, nx)
     packing = strip_plan(ny, nx)
     f32 = jnp.float32
+    send_y, send_x, send_z, send_cy, send_cx, send_cd, send_cz = (in_sem.at[i] for i in (0, 1, 4, 5, 6, 2, 3))
 
     def exists(dy, dx):
         ok = None
@@ -106,10 +107,10 @@
     for cond, refs in (
         (iz == 0, [u.at[:, 0, own]]),
         (iz == ngz - 1, [u.at[:, nz + 1, own]]),
-        (iy == 0, [yrecv.at[:, 0], cyrecv.at[0], lrecv.at[0]]),
-        (iy == ngy - 1, [yrecv.at[:, 1], cyrecv.at[1], lrecv.at[1]]),
-        (ix == 0, [xrecv.at[:, 0], cxrecv.at[0], vrecv.at[0]]),
-        (ix == ngx - 1, [xrecv.at[:, 1], cxrecv.at[1], vrecv.at[1]]),
+        (iy == 0, [yrecv.at[:, 0], cyrecv.at[0]]),
+        (iy == ngy - 1, [yrecv.at[:, 1], cyrecv.at[1]]),
+        (ix == 0, [xrecv.at[:, 0], cxrecv.at[0]]),
+        (ix == ngx - 1, [xrecv.at[:, 1], cxrecv.at[1]]),
         (jnp.logical_or(iy == 0, ix == 0), [cdrecv.at[0]]),
         (jnp.logical_or(iy == 0, ix == ngx - 1), [cdrecv.at[1]]),
         (jnp.logical_or(iy == ngy - 1, ix == 0), [cdrecv.at[2]]),
@@ -187,20 +188,20 @@
                 copy.start()
 
     def y_copies(batch):
-        s = h_send.at[2 + batch], h_recv.at[2 + batch]
+        s = send_y, h_recv.at[1 + batch]
         return [(exists(1, 0), remote(ysend.at[batch, 1], yrecv.at[batch, 0], *s, at(1, 0))),
                 (exists(-1, 0), remote(ysend.at[batch, 0], yrecv.at[batch, 1], *s, at(-1, 0)))]
 
     def x_copies(batch):
-        s = h_send.at[4 + batch], h_recv.at[4 + batch]
+        s = send_x, h_recv.at[3 + batch]
         return [(exists(0, 1), remote(xsend.at[batch], xrecv.at[batch, 0], *s, at(0, 1))),
                 (exists(0, -1), remote(xsend.at[batch], xrecv.at[batch, 1], *s, at(0, -1)))]
 
     def z_device(d):
         return {"gx": ix, "gy": iy, "gz": iz + d}
 
-    z_up = remote(u.at[:, nz, own], u.at[:, 0, own], h_send.at[0], h_recv.at[0], z_device(1))
-    z_down = remote(u.at[:, 1, own], u.at[:, nz + 1, own], h_send.at[1], h_recv.at[1], z_device(-1))
+    z_up = remote(u.at[:, nz, own], u.at[:, 0, own], send_z, h_recv.at[0], z_device(1))
+    z_down = remote(u.at[:, 1, own], u.at[:, nz + 1, own], send_z, h_recv.at[0], z_device(-1))
     has_below, has_above = iz > 0, iz < ngz - 1
 
     start(y_copies(0))
@@ -222,11 +223,14 @@
         counted(count, cases, lambda ref: remote(ref, ref, send, recv, z_device(0)),
                 (lambda c: c.wait_send()) if sent else (lambda c: c.wait_recv()))
 
-    def wait_y(batch, sent):
-        wait_many(beside_y, ((1, yrecv.at[batch, 0]), (2, yrecv.at[batch])), h_send.at[2 + batch], h_recv.at[2 + batch], sent)
-
-    def wait_x(batch, sent):
-        wait_many(beside_x, ((1, xrecv.at[batch, 0]), (2, xrecv.at[batch])), h_send.at[4 + batch], h_recv.at[4 + batch], sent)
+    def wait_y(batch):
+        wait_many(beside_y, ((1, yrecv.at[batch, 0]), (2, yrecv.at[batch])), send_y, h_recv.at[1 + batch], False)
+
+    def wait_x(batch):
+        wait_many(beside_x, ((1, xrecv.at[batch, 0]), (2, xrecv.at[batch])), send_x, h_recv.at[3 + batch], False)
+
+    beside_z = has_below.astype(jnp.int32) + has_above.astype(jnp.int32)
+    z_cases = ((1, u.at[:, 1, own]), (2, u.at[:, 1:3, own]))
 
     for i in range(2):
         values = []
@@ -314,13 +318,7 @@
         p_rhs.append(s_res[g] - s_z[g] - (s_hx[g] - pltpu.roll(s_hx[g], 1, 1)) - (s_hy[g] - shifted[0, padded(g, -1), :]))
         p_dia.append(s_dia[g] + s_ty[g] + shifted[1, padded(g, -1), :] + s_tx[g] + pltpu.roll(s_tx[g], 1, 1))
 
-    @pl.when(has_below)
-    def _():
-        z_up.wait_recv()
-
-    @pl.when(has_above)
-    def _():
-        z_down.wait_recv()
+    wait_many(beside_z, z_cases, send_z, h_recv.at[0], False)
     for slot, z, inside in ((0, 0, 1), (nz + 1, nz - 1, nz)):
         k0 = [coefficient(ktab, z, 0, k) for k in range(3)]
         for g in range(groups):
@@ -350,43 +348,33 @@
 
     pl.semaphore_wait(far_sem, ngz - 1)
 
-    def to_all(dy, dx, src, dst, sem):
-        return [(exists(dy, dx), remote(src, dst, c_send.at[sem], c_recv.at[sem],
+    def to_all(dy, dx, src, dst, send, recv):
+        return [(exists(dy, dx), remote(src, dst, send, c_recv.at[recv],
                                         {"gx": ix + dx, "gy": iy + dy, "gz": lax.rem(iz + d, ngz)})) for d in range(ngz)]
 
+    nstrips = len(packing)
     for dy, dx in SIDES[4:]:
-        start(to_all(dy, dx, strips.at[0 if dy < 0 else last_head], cdrecv.at[(1 - dy) + (1 - dx) // 2, iz], 3))
+        start(to_all(dy, dx, strips.at[0 if dy < 0 else last_head], cdrecv.at[(1 - dy) + (1 - dx) // 2, iz], send_cd, 3))
     for dx in (-1, 1):
-        start(to_all(0, dx, strips, cxrecv.at[(1 - dx) // 2, iz], 2))
+        start(to_all(0, dx, strips, cxrecv.at[(1 - dx) // 2, iz, 0:nstrips], send_cx, 2))
     for dy in (-1, 1):
-        start(to_all(dy, 0, ystrips.at[(1 + dy) // 2], cyrecv.at[(1 - dy) // 2, iz], 1))
-
-    wait_y(0, False)
+        start(to_all(dy, 0, ystrips.at[(1 + dy) // 2], cyrecv.at[(1 - dy) // 2, iz, 0:PLANES], send_cy, 1))
+
+    wait_y(0)
     top8, bottom8 = row8 == 0, row8 == HALO - 1
     lines = nil8
-    for side, g, here, beyond in ((0, 0, top8, bottom8), (1, groups - 1, bottom8, top8)):
+    y_faces = []
+    for side, g, here in ((0, 0, top8), (1, groups - 1, bottom8)):
         there = yrecv[0, side, nz:, :]
         t = jnp.where(there > 0.0, 1.0 / (ysend[0, side, nz:, :] + there), 0.0)
         moved = jnp.sum(t * (ysend[0, side, :nz, :] - yrecv[0, side, :nz, :]), axis=0, keepdims=True)
         weight = jnp.sum(rowk[0] * t, axis=0, keepdims=True)
-        changes = [jnp.where(here, -moved, jnp.where(beyond, moved, 0.0)),
-                   jnp.where(jnp.logical_or(here, beyond), weight, 0.0),
-                   jnp.where(bottom8, weight, 0.0)]
-        packed = nil8
-        for p in range(3):
-            packed = jnp.where(group8 == p, pltpu.roll(changes[p], 2 * HALO * p + HALO, 1), packed)
-        vsend[side] = packed
-        for z in range(nz):
-            edge_row = HALO - 1 + side * ny
-            ty[z, edge_row:edge_row + 1, :] = t[z:z + 1]
-        for p in range(3 if side else 2):
-            planes[p][g] = planes[p][g] + jnp.where(here, changes[p], 0.0)
         lines = jnp.where(row8 == 2 * side, moved, jnp.where(row8 == 2 * side + 1, weight, lines))
-    zplanes[iz, PLANES * groups] = lines
+        y_faces.append((side, g, here, t, moved, weight))
+    vsend[...] = lines
     for dx in (-1, 1):
-        start(to_all(0, dx, vsend, vrecv.at[(1 - dx) // 2, iz], 4))
-
-    wait_x(0, False)
+        start(to_all(0, dx, vsend, cxrecv.at[(1 - dx) // 2, iz, nstrips], send_cx, 4))
+    wait_x(0)
     flux, weights, faces, outside = [], [], [], []
     for t in range(xtiles):
         there = [jnp.where(even8, xrecv[0, 0, i, t], xrecv[0, 1, i, t]) for i in range(2)]
@@ -395,45 +383,62 @@
         weights.append(face * lanek[0])
         faces.append(face)
         outside.append(there[0])
+
+    def side_sums(g):
+        low = (g % per) * 2 * nz
+        block = jnp.logical_and(lane8 >= low, lane8 < low + 2 * nz)
+        sums = []
+        for values in (flux, weights):
+            for parity in (even8, jnp.logical_not(even8)):
+                chosen = jnp.where(jnp.logical_and(block, parity), values[g // per], 0.0)
+                sums.append(jnp.sum(chosen, axis=1, keepdims=True))
+        return sums
+
+    def at_sides(left, right):
+        return jnp.where(first8, left, jnp.where(last8, right, 0.0))
+
+    sums = {}
+    for side, g in ((0, 0), (1, groups - 1)):
+        if g not in sums:
+            sums[g] = side_sums(g)
+        flux_l, flux_r, weight_l, weight_r = sums[g]
+        tile = nil8
+        for i, column in enumerate((-flux_r, -flux_l, weight_r, weight_l, flux_l, flux_r, weight_l, weight_r)):
+            tile = jnp.where(lane8 == i, column, tile)
+        lsend[side] = tile
+    for dy in (-1, 1):
+        start(to_all(dy, 0, lsend.at[(1 + dy) // 2], cyrecv.at[(1 - dy) // 2, iz, PLANES], send_cy, 5))
+
+    for side, g, here, t, moved, weight in y_faces:
+        for p, change in ((0, -moved), (1, weight), (2, weight))[:3 if side else 2]:
+            planes[p][g] = planes[p][g] + jnp.where(here, change, 0.0)
+        for z in range(nz):
+            edge_row = HALO - 1 + side * ny
+            ty[z, edge_row:edge_row + 1, :] = t[z:z + 1]
+    zplanes[iz, PLANES * groups] = lines
     in16 = lax.rem(lane8, 2 * HALO)
     for i, tiles in enumerate(packing):
         across = nil8
         for j, g in enumerate(tiles):
-            low = (g % per) * 2 * nz
-            block = jnp.logical_and(lane8 >= low, lane8 < low + 2 * nz)
-            sums = []
-            for values in (flux, weights):
-                for parity in (even8, jnp.logical_not(even8)):
-                    chosen = jnp.where(jnp.logical_and(block, parity), values[g // per], 0.0)
-                    sums.append(jnp.sum(chosen, axis=1, keepdims=True))
-            flux_l, flux_r, weight_l, weight_r = sums
-            changes = [jnp.where(first8, -flux_l, jnp.where(last8, -flux_r, 0.0)),
-                       jnp.where(first8, weight_l, jnp.where(last8, weight_r, 0.0)),
-                       jnp.where(last8, weight_r, 0.0)]
-            for p, change in zip((0, 1, 3), changes):
+            if g not in sums:
+                sums[g] = side_sums(g)
+            flux_l, flux_r, weight_l, weight_r = sums[g]
+            for p, change in ((0, at_sides(-flux_l, -flux_r)), (1, at_sides(weight_l, weight_r)),
+                              (3, jnp.where(last8, weight_r, 0.0))):
                 planes[p][g] = planes[p][g] + change
             for p, left, right in ((0, flux_l, flux_r), (1, weight_l, weight_r), (3, weight_l, 0.0)):
                 slot = (j * PLANES + p) * 2 * HALO
                 across = jnp.where(lane8 == slot + HALO - 1, left, jnp.where(lane8 == slot + HALO, right, across))
-            for side, head in ((0, 0), (1, groups - 1)):
-                if g == head:
-                    for n in range(3):
-                        lsend[side, n] = changes[n]
         zplanes[iz, PLANES * groups + 1 + i] = across
-        for side, head in ((0, 0), (1, last_head)):
-            if i == head:
-                lsend[side, 3] = across
-    for dy in (-1, 1):
-        start(to_all(dy, 0, lsend.at[(1 + dy) // 2], lrecv.at[(1 - dy) // 2, iz], 5))
     for p in range(PLANES):
         for g in range(groups):
             zplanes[iz, p * groups + g] = planes[p][g]
     for d in range(1, ngz):
-        remote(zplanes.at[iz], zplanes.at[iz], c_send.at[0], c_recv.at[0],
+        remote(zplanes.at[iz], zplanes.at[iz], send_cz, c_recv.at[0],
                {"gx": ix, "gy": iy, "gz": lax.rem(iz + d, ngz)}).start()
 
-    wait_y(1, False)
-    wait_x(1, False)
+    wait_y(1)
+    wait_x(1)
     invrow = 1.0 / rowk[0]
     for side, at_row in ((0, HALO - 1), (1, HALO + ny)):
         one, two_ = yrecv[1, side, :nz, :], yrecv[1, side, nz:, :]
@@ -501,17 +506,11 @@
     corners = beside_y * beside_x
     if ngz > 1:
         others = zplanes.at[0:ngz - 1]
-        remote(others, others, c_send.at[0], c_recv.at[0], z_device(0)).wait_recv()
-    y_cases = ((1, cyrecv.at[0]), (2, cyrecv))
-    x_cases = ((1, cxrecv.at[0]), (2, cxrecv))
+        remote(others, others, send_cz, c_recv.at[0], z_device(0)).wait_recv()
     d_cases = ((1, cdrecv.at[0]), (2, cdrecv.at[0:2]), (4, cdrecv))
-    wait_many(beside_y, y_cases, c_send.at[1], c_recv.at[1], False)
-    wait_many(beside_x, x_cases, c_send.at[2], c_recv.at[2], False)
-    wait_many(corners, d_cases, c_send.at[3], c_recv.at[3], False)
-    v_cases = ((1, vrecv.at[0]), (2, vrecv))
-    l_cases = ((1, lrecv.at[0]), (2, lrecv))
-    wait_many(beside_x, v_cases, c_send.at[4], c_recv.at[4], False)
-    wait_many(beside_y, l_cases, c_send.at[5], c_recv.at[5], False)
+    wait_many(beside_y, ((1, cyrecv.at[0, :, 0:PLANES]), (2, cyrecv.at[:, :, 0:PLANES])), send_cy, c_recv.at[1], False)
+    wait_many(beside_x, ((1, cxrecv.at[0, :, 0:nstrips]), (2, cxrecv.at[:, :, 0:nstrips])), send_cx, c_recv.at[2], False)
+    wait_many(corners, d_cases, send_cd, c_recv.at[3], False)
 
     def gathered(part):
         total = part(0)
@@ -519,32 +518,15 @@
             total = total + part(i)
         return total
 
-    rows = ny + 2 * HALO
-    elane = lax.broadcasted_iota(jnp.int32, (rows, nx), 1)
-    efirst, elast = elane == 0, elane == nx - 1
+    tiles_in = groups + 2
     left_part = in16 < HALO
-    lines = gathered(lambda i: zplanes[i, PLANES * groups])
-    late = [jnp.where(left_part, gathered(lambda i: vrecv[0, i, v]), gathered(lambda i: vrecv[1, i, v])) for v in range(2)]
-    beside = [[gathered(lambda i: lrecv[side, i, n]) for n in range(4)] for side in range(2)]
     side_tiles = [jnp.where(left_part, gathered(lambda i: cxrecv[0, i, t]), gathered(lambda i: cxrecv[1, i, t]))
-                  + gathered(lambda i: zplanes[i, PLANES * groups + 1 + t]) for t in range(len(packing))]
-    side_tiles[0] = side_tiles[0] + jnp.where(top8, late[0], 0.0)
-    side_tiles[last_head] = side_tiles[last_head] + jnp.where(bottom8, late[1], 0.0)
+                  + gathered(lambda i: zplanes[i, PLANES * groups + 1 + t]) for t in range(nstrips)]
     corner_tiles = [jnp.where(left_part, gathered(lambda i: cdrecv[2 * v, i]), gathered(lambda i: cdrecv[2 * v + 1, i]))
-                    + jnp.where(bottom8 if v == 0 else top8, late[v], 0.0) + beside[v][3] for v in range(2)]
-    end_tiles = []
-    for side, here in ((0, bottom8), (1, top8)):
-        moved, weight = lines[2 * side:2 * side + 1], lines[2 * side + 1:2 * side + 2]
-        tiles = [gathered(lambda i: cyrecv[side, i, p]) for p in range(PLANES)]
-        for n, p in enumerate((0, 1, 3)):
-            tiles[p] = tiles[p] + beside[side][n]
-        tiles[0] = tiles[0] + jnp.where(here, moved, 0.0)
-        tiles[1] = tiles[1] + jnp.where(here, weight, 0.0)
-        if side == 0:
-            tiles[2] = tiles[2] + jnp.where(here, weight, 0.0)
-        end_tiles.append(tiles)
+                    for v in range(2)]
     where_is = {g: (i, j) for i, tiles in enumerate(packing) for j, g in enumerate(tiles)}
-    strip8 = jnp.logical_or(lane8 < HALO, lane8 >= nx - HALO)
+    on_right, on_left = lane8 < HALO, lane8 >= nx - HALO
+    strip8 = jnp.logical_or(on_right, on_left)
 
     def border_of(p, g):
         if 0 <= g < groups:
@@ -554,61 +536,104 @@
             tile, slot = corner_tiles[0 if g < 0 else 1], p
         return jnp.where(strip8, pltpu.roll(tile, (2 * nx - 2 * HALO * slot - HALO) % nx, 1), 0.0)
 
-    b = [jnp.concatenate([border_of(p, g) for g in range(-1, groups + 1)], axis=0) for p in range(PLANES)]
-    a = [jnp.concatenate([end_tiles[0][p]] + [gathered(lambda i: zplanes[i, p * groups + g]) for g in range(groups)]
-                         + [end_tiles[1][p]], axis=0) for p in range(PLANES)]
-
-    def east(a, b):
-        ra, rb = pltpu.roll(a, nx - 1, 1), pltpu.roll(b, nx - 1, 1)
-        return jnp.where(elast, rb, ra), jnp.where(elast, ra, rb)
-
-    def west(a, b):
-        ra, rb = pltpu.roll(a, 1, 1), pltpu.roll(b, 1, 1)
-        return jnp.where(efirst, rb, ra), jnp.where(efirst, ra, rb)
-
-    mid = slice(HALO, HALO + rows)
-    wests = west(a[3], b[3])
-    terms = []
-    for s, planes_ in enumerate((a, b)):
-        there = planes_[1] > 0.0
-        inv = jnp.where(there, RELAX / jnp.where(there, planes_[1], 1.0), 0.0)
-        field[s, mid, :] = planes_[2]
-        south = field[s, HALO - 1:HALO - 1 + rows, :]
-        terms.append((planes_[0] * inv, planes_[2] * inv, south * inv, planes_[3] * inv, wests[s] * inv))
-
-    c = [terms[0][0], terms[1][0]]
+    b = [[border_of(p, g) for g in range(-1, groups + 1)] for p in range(PLANES)]
+    own_lines = gathered(lambda i: zplanes[i, PLANES * groups])
+    a = [[gathered(lambda i: cyrecv[0, i, p])] + [gathered(lambda i: zplanes[i, p * groups + g]) for g in range(groups)]
+         + [gathered(lambda i: cyrecv[1, i, p])] for p in range(PLANES)]
+
+    def beyond(grid, lines):
+        for side, t, here in ((0, 0, bottom8), (1, tiles_in - 1, top8)):
+            moved, weight = lines[2 * side:2 * side + 1], lines[2 * side + 1:2 * side + 2]
+            for p, change in ((0, moved), (1, weight), (2, weight))[:2 if side else 3]:
+                grid[p][t] = grid[p][t] + jnp.where(here, change, 0.0)
+
+    beyond(a, own_lines)
+
+    def east(ra, rb):
+        return jnp.where(last8, rb, ra), jnp.where(last8, ra, rb)
+
+    def west(ra, rb):
+        return jnp.where(first8, rb, ra), jnp.where(first8, ra, rb)
+
+    def fill(buffer, s, tiles):
+        for t in range(tiles_in):
+            field[buffer, s, (t + 1) * HALO:(t + 2) * HALO, :] = tiles[t]
+
+    def above(buffer, s, t):
+        return field[buffer, s, (t + 1) * HALO - 1:(t + 2) * HALO - 1, :]
+
+    def below(buffer, s, t):
+        return field[buffer, s, (t + 1) * HALO + 1:(t + 2) * HALO + 1, :]
+
+    terms = [[None] * tiles_in for _ in range(2)]
+    grids = (a, b)
+
+    def prepare(s, t):
+        rhs_, dia, down, right = (grids[s][p][t] for p in range(PLANES))
+        there = dia > 0.0
+        inv = jnp.where(there, RELAX / jnp.where(there, dia, 1.0), 0.0)
+        left = west(*(pltpu.roll(grid[3][t], 1, 1) for grid in grids))[s]
+        terms[s][t] = [rhs_ * inv, down * inv, above(0, s, t) * inv, right * inv, left * inv]
+
+    fill(0, 0, a[2])
+    late_b = (0, 1, groups, groups + 1)
+    for t in range(1, tiles_in - 1):
+        prepare(0, t)
+
+    wait_many(beside_x, ((1, cxrecv.at[0, :, nstrips]), (2, cxrecv.at[:, :, nstrips])), send_cx, c_recv.at[4], False)
+    lines = jnp.where(on_left, gathered(lambda i: cxrecv[0, i, nstrips]),
+                      jnp.where(on_right, gathered(lambda i: cxrecv[1, i, nstrips]), 0.0))
+    beyond(b, lines)
+    for side, t, here in ((0, 1, top8), (1, groups, bottom8)):
+        moved, weight = lines[2 * side:2 * side + 1], lines[2 * side + 1:2 * side + 2]
+        for p, change in ((0, -moved), (1, weight), (2, weight))[:3 if side else 2]:
+            b[p][t] = b[p][t] + jnp.where(here, change, 0.0)
+    fill(0, 1, b[2])
+    for t in range(1, tiles_in - 1):
+        prepare(1, t)
+    wait_many(beside_y, ((1, cyrecv.at[0, :, PLANES]), (2, cyrecv.at[:, :, PLANES])), send_cy, c_recv.at[5], False)
+    for side, t in ((0, 0), (1, tiles_in - 1)):
+        columns = gathered(lambda i: cyrecv[side, i, PLANES])
+        flux_, weight_, flux_past, weight_past = (
+            jnp.where(outer8, pltpu.roll(columns, nx - 2 * n - 1, 1), 0.0) for n in range(4))
+        for grid, change, weight in ((a, flux_, weight_), (b, flux_past, weight_past)):
+            grid[0][t] = grid[0][t] + change
+            grid[1][t] = grid[1][t] + weight
+            grid[3][t] = grid[3][t] + jnp.where(last8, weight, 0.0)
+        for s in range(2):
+            prepare(s, t)
+
+    c = [[terms[s][t][0] for t in range(tiles_in)] for s in range(2)]
     for sweep in range(1, SWEEPS):
-        e, ws = east(*c), west(*c)
+        buffer = sweep % 2
         for s in range(2):
-            field[s, mid, :] = c[s]
-        nxt = []
-        for s in range(2):
-            r, tyn, tys, txe, txw = terms[s]
-            nxt.append((1.0 - RELAX) * c[s] + r
-                       + tyn * field[s, HALO + 1:HALO + 1 + rows, :] + tys * field[s, HALO - 1:HALO - 1 + rows, :]
-                       + txe * e[s] + txw * ws[s])
+            fill(buffer, s, c[s])
+        nxt = [[None] * tiles_in for _ in range(2)]
+        for t in range(tiles_in):
+            e = east(*(pltpu.roll(c[s][t], nx - 1, 1) for s in range(2)))
+            ws = west(*(pltpu.roll(c[s][t], 1, 1) for s in range(2)))
+            for s in range(2):
+                r, tyn, tys, txe, txw = terms[s][t]
+                nxt[s][t] = (((1.0 - RELAX) * c[s][t] + r) + (tyn * below(buffer, s, t) + tys * above(buffer, s, t))
+                             + (txe * e[s] + txw * ws[s]))
         c = nxt
-    e, ws = east(*c), west(*c)
-    final[0] = c[0]
-    final[1] = e[0]
-    final[2] = ws[0]
-    @pl.when(has_above)
-    def _():
-        z_up.wait_send()
-
-    @pl.when(has_below)
-    def _():
-        z_down.wait_send()
-    for batch in range(2):
-        wait_y(batch, True)
-        wait_x(batch, True)
+    for t in range(tiles_in):
+        rows = slice(t * HALO, (t + 1) * HALO)
+        final[0, rows, :] = c[0][t]
+        if 0 < t < tiles_in - 1:
+            final[1, rows, :] = east(*(pltpu.roll(c[s][t], nx - 1, 1) for s in range(2)))[0]
+            final[2, rows, :] = west(*(pltpu.roll(c[s][t], 1, 1) for s in range(2)))[0]
+    for count, cases, sem in (
+        (beside_y, ((1, yrecv.at[0]), (2, yrecv)), send_y),
+        (beside_x, ((1, xrecv.at[0]), (2, xrecv)), send_x),
+        (beside_z, z_cases, send_z),
+        (beside_y, ((1, cyrecv.at[0]), (2, cyrecv)), send_cy),
+        (beside_x, ((1, cxrecv.at[0]), (2, cxrecv)), send_cx),
+        (corners, d_cases, send_cd),
+    ):
+        wait_many(count, cases, sem, h_recv.at[0], True)
     if ngz > 1:
-        remote(others, others, c_send.at[0], c_recv.at[0], z_device(0)).wait_send()
-    wait_many(beside_y, y_cases, c_send.at[1], c_recv.at[1], True)
-    wait_many(beside_x, x_cases, c_send.at[2], c_recv.at[2], True)
-    wait_many(corners, d_cases, c_send.at[3], c_recv.at[3], True)
-    wait_many(beside_x, v_cases, c_send.at[4], c_recv.at[4], True)
-    wait_many(beside_y, l_cases, c_send.at[5], c_recv.at[5], True)
+        remote(others, others, send_cz, c_recv.at[0], z_device(0)).wait_send()
 
 
 def finish_kernel(parts, w, qv, tzs, ty, txp, txm, final, new_hbm, corr_hbm, out, out_sem):
@@ -666,12 +691,11 @@
             vmem(2, 2, xtiles, HALO, nx), vmem(2, 2, 2, xtiles, HALO, nx), vmem(4, xtiles, HALO, nx),
             vmem(3, nz, nx), vmem(nz + 1, ny, nx), vmem(2, ey, nx),
             vmem(ngz, PLANES * groups + 1 + strips, HALO, nx), vmem(2, PLANES, HALO, nx), vmem(strips, HALO, nx),
-            vmem(2, ngz, PLANES, HALO, nx), vmem(2, ngz, strips, HALO, nx), vmem(4, ngz, HALO, nx),
-            vmem(2, HALO, nx), vmem(2, ngz, 2, HALO, nx), vmem(2, 4, HALO, nx), vmem(2, ngz, 4, HALO, nx),
-            vmem(2, ey + 2 * HALO, nx),
+            vmem(2, ngz, PLANES + 1, HALO, nx), vmem(2, ngz, strips + 1, HALO, nx), vmem(4, ngz, HALO, nx),
+            vmem(HALO, nx), vmem(2, HALO, nx), vmem(2, 2, ey + 2 * HALO, nx),
             pltpu.SMEM((nz,), facies.dtype), pltpu.SMEM((3, facets, 3), f32), pltpu.SMEM((3, facets, 3), f32),
             pltpu.SMEM((NCOEF, facets), f32),
-            pltpu.SemaphoreType.REGULAR, pltpu.SemaphoreType.REGULAR, dma(7), dma(6), dma(6), dma(6), dma(6),
+            pltpu.SemaphoreType.REGULAR, pltpu.SemaphoreType.REGULAR, dma(7), dma(5), dma(6),
         ],
         compiler_params=pltpu.CompilerParams(collective_id=0, has_side_effects=True, vmem_limit_bytes=limit),
         name="cpr_apply",

time: 12.9 us -> 12.4 us (0.961)
  Pallas kernels: 12.1 us -> 11.6 us
    pallas_call x1, Pallas kernels: 11 us -> 10.6 us  [per_device(): pl.pallas_call(functools.partial(kernel, sizes), out_shape=(vmem(3, *cell...]
where the time goes in v2:
time: 12.4 us; the launch traced here: 12.3 us
  Pallas kernels  11.6 us (94%)
  between operations  0.64 us (5%)
    pallas_call x1, Pallas kernels, per_device(): pl.pallas_call(functools.partial(kernel, sizes), out_shape=(vmem(3, *cell...  10.6 us
    pallas_call x1, Pallas kernels, per_device(): pl.pallas_call(functools.partial(finish_kernel, parts), out_shape=(jax.Sh...  1.05 us

profile of v2, /device:TPU:0, one launch (start us, length us, event | category | flops | bytes accessed | tf_op | source)
XLA Modules:
  0.0 12.3 jit_solution(10368152859644945041)
XLA Ops:
  0.6 10.6 %cpr_apply.1 = (f32[3,16,40,128]{3,2,1,0:T(8,128)S(1)}, f32[3,16,40,128]{3,2,1,0:T(8,128)S(1)}, f32[16,40,128]{2,1,0:T(8,128)S(1)}, f32[16,56,128]{2,1,0:T(8,128...) custom-call(s32[16]{0:T(128)} %facies_hbm.1, f32[3,4,3]{2,1,0:T(4,128)} %bitcast.2, ...), custom_call_target="tpu_custom_call" | custom-call | tf_op jit(solution)/shard_map/cpr_apply/pallas_call | solution.py:681
  11.2 1.0 %cpr_finish.1 = (f32[3,16,40,128]{3,2,1,0:T(8,128)}, f32[40,128]{1,0:T(8,128)}) custom-call(f32[3,16,40,128]{3,2,1,0:T(8,128)S(1)} %get-tuple-element.9.w, f32[3,16,40,128]{3,2,1,0:T(8,128)S(1)} %get-tuple-element.10.qv, f32[16,40,128]{2,1,0:T(8,128)S(1)} %get-tuple-element.11.tzs, f32[16,56,128]{2,1,0:T(8,128)S(1)} %get-tuple-element.12.ty, ...), custom_call_target="tpu_custom_call" | custom-call | tf_op jit(solution)/shard_map/cpr_finish/pallas_call | solution.py:705

commit v3 on v2

--- a/solution.py
+++ b/solution.py
@@ -55,13 +55,18 @@
 def kernel(sizes, facies_hbm, mtab_hbm, ktab_hbm, state_hbm, rhs_hbm, perm_hbm, pore_hbm,
            w, qv, tzs, ty, txp, txm, final,
            u, pcb, rhs, permb, poreb, ysend, yrecv, xsend, xrecv, edge, rowk, tzf, shifted,
-           zplanes, ystrips, strips, cyrecv, cxrecv, cdrecv, vsend, lsend, field,
-           facies, mtab, ktab, ctab, near_sem, far_sem, in_sem, h_recv, c_recv):
+           zplanes, ystrips, strips, cyrecv, cxrecv, cdrecv, rpsend, dsend, field,
+           facies, mtab, ktab, ctab, near, far_sem, in_sem, h_recv, c_recv):
     ngx, ngy, ngz, nz, ny, nx = sizes
     ix, iy, iz = lax.axis_index("gx"), lax.axis_index("gy"), lax.axis_index("gz")
     own = slice(HALO, HALO + ny)
     groups, per, xtiles = column_plan(nz, ny, nx)
     packing = strip_plan(ny, nx)
+    nstrips = len(packing)
+    last_head = len(packing[:2]) - 1
+    layers = nz // HALO
+    ends = ((0, 0), (1, groups - 1))
+    first_part = PLANES * groups + 1 + nstrips
     f32 = jnp.float32
     send_y, send_x, send_z, send_cy, send_cx, send_cd, send_cz = (in_sem.at[i] for i in (0, 1, 4, 5, 6, 2, 3))
 
@@ -77,7 +82,7 @@
         return {"gx": ix + dx, "gy": iy + dy, "gz": iz}
 
     barrier = pltpu.get_barrier_semaphore()
-    for side in (SIDES[2], SIDES[3], SIDES[0], SIDES[1]):
+    for side in (SIDES[0], SIDES[2], SIDES[1], SIDES[3]):
         @pl.when(exists(*side))
         def _(side=side):
             pl.semaphore_signal(barrier, inc=1, device_id=at(*side), device_id_type=MESH)
@@ -137,6 +142,9 @@
     even8 = lax.rem(lane8, 2) == 0
     first8, last8 = lane8 == 0, lane8 == nx - 1
     nil8 = jnp.zeros((HALO, nx), f32)
+    group8 = lax.shift_right_logical(lane8, 4)
+    in16 = lax.rem(lane8, 2 * HALO)
+    left_part = in16 < HALO
 
     def packed_columns(values):
         out = [nil8] * xtiles
@@ -207,11 +215,11 @@
     start(y_copies(0))
     start(x_copies(0))
     start([(has_above, z_up), (has_below, z_down)])
-    for side in SIDES[:4]:
-        @pl.when(exists(*side))
-        def _(side=side):
-            pl.semaphore_signal(near_sem, inc=1, device_id=at(*side), device_id_type=MESH)
-    signal_peers(near_sem)
+    for n, dy in ((1, -1), (0, 1)):
+        @pl.when(exists(dy, 0))
+        def _(n=n, dy=dy):
+            pl.semaphore_signal(near.at[n], inc=1, device_id=at(dy, 0), device_id_type=MESH)
+    signal_peers(near.at[2])
 
     def counted(count, cases, descriptor, done):
         for n, ref in cases:
@@ -244,12 +252,42 @@
             xsend[1, i, t] = packed[t]
     start(x_copies(1))
     start(y_copies(1))
-
-    for f in range(ktab.shape[1]):
-        values = block_scalars([[mtab[r, f, c] for c in range(3)] for r in range(3)],
-                               [[ktab[r, f, c] for c in range(3)] for r in range(3)])
-        for i, value in enumerate(values):
-            ctab[i, f] = value
+    for i in range(2):
+        here, swap = nil8, nil8
+        for side in range(2):
+            for k in range(layers):
+                rows = slice(i * nz + k * HALO, i * nz + (k + 1) * HALO)
+                for other in range(2):
+                    slot = (side if not other else 1 - side) * layers + k
+                    moved = pltpu.roll(ysend[0, side, rows, :], (2 * HALO * slot + HALO) % nx, 1)
+                    if other:
+                        swap = jnp.where(group8 == slot, moved, swap)
+                    else:
+                        here = jnp.where(group8 == slot, moved, here)
+        rpsend[i] = here
+        for side, g in ends:
+            dsend[side, i] = swap
+            dsend[side, 2 + i] = xsend[0, i, g // per]
+
+    def ways(dy, dx, copy):
+        @pl.when(exists(dy, dx))
+        def _():
+            copy.start()
+
+    for dx in (-1, 1):
+        ways(0, dx, remote(rpsend, cxrecv.at[(1 - dx) // 2, ngz * nstrips:], send_cx, h_recv.at[5], at(0, dx)))
+    for dy in (-1, 1):
+        ways(dy, 0, remote(dsend.at[(1 + dy) // 2, 2:], cyrecv.at[(1 - dy) // 2, ngz * PLANES:], send_cy, h_recv.at[5], at(dy, 0)))
+
+    def raw_corners(dy):
+        @pl.when(exists(dy, 0))
+        def _():
+            pl.semaphore_wait(near.at[(1 + dy) // 2], 1)
+        for dx in (-1, 1):
+            ways(dy, dx, remote(dsend.at[(1 + dy) // 2], cdrecv.at[(1 - dy) + (1 - dx) // 2, ngz:], send_cd, h_recv.at[6],
+                                at(dy, dx)))
+
+
     layer_of_lane = lax.rem(lane8[0:1], 2 * nz) // 2
     lanek = [jnp.zeros((1, nx), f32) for _ in range(3)]
     for z in range(nz):
@@ -257,9 +295,16 @@
             value = coefficient(ktab, z, 0, k)
             rowk[k, z:z + 1, :] = jnp.full((1, nx), value, f32)
             lanek[k] = jnp.where(layer_of_lane == z, value, lanek[k])
-
     loads[2].wait()
     loads[3].wait()
+
+    raw_corners(-1)
+
+    for f in range(ktab.shape[1]):
+        values = block_scalars([[mtab[r, f, c] for c in range(3)] for r in range(3)],
+                               [[ktab[r, f, c] for c in range(3)] for r in range(3)])
+        for i, value in enumerate(values):
+            ctab[i, f] = value
 
     def tile_of(g):
         return slice(g * HALO, (g + 1) * HALO)
@@ -329,12 +374,11 @@
             d = [u[k, inside, rows, :] - u[k, slot, rows, :] for k in range(3)]
             p_rhs[g] = p_rhs[g] - t * (k0[0] * d[0] + k0[1] * d[1] + k0[2] * d[2])
     mine = [[swapped(xsend[0, i, t]) for t in range(xtiles)] for i in range(2)]
-    pl.semaphore_wait(near_sem, beside_y + beside_x + (ngz - 1))
+    raw_corners(1)
+    pl.semaphore_wait(near.at[2], ngz - 1)
     signal_peers(far_sem)
 
     planes = [p_rhs, p_dia, s_ty, s_tx]
-    group8 = lax.shift_right_logical(lane8, 4)
-    last_head = len(packing[:2]) - 1
     for p in range(PLANES):
         ystrips[0, p] = planes[p][0]
         ystrips[1, p] = planes[p][groups - 1]
@@ -352,13 +396,12 @@
         return [(exists(dy, dx), remote(src, dst, send, c_recv.at[recv],
                                         {"gx": ix + dx, "gy": iy + dy, "gz": lax.rem(iz + d, ngz)})) for d in range(ngz)]
 
-    nstrips = len(packing)
     for dy, dx in SIDES[4:]:
         start(to_all(dy, dx, strips.at[0 if dy < 0 else last_head], cdrecv.at[(1 - dy) + (1 - dx) // 2, iz], send_cd, 3))
     for dx in (-1, 1):
-        start(to_all(0, dx, strips, cxrecv.at[(1 - dx) // 2, iz, 0:nstrips], send_cx, 2))
+        start(to_all(0, dx, strips, cxrecv.at[(1 - dx) // 2, pl.ds(iz * nstrips, nstrips)], send_cx, 2))
     for dy in (-1, 1):
-        start(to_all(dy, 0, ystrips.at[(1 + dy) // 2], cyrecv.at[(1 - dy) // 2, iz, 0:PLANES], send_cy, 1))
+        start(to_all(dy, 0, ystrips.at[(1 + dy) // 2], cyrecv.at[(1 - dy) // 2, pl.ds(iz * PLANES, PLANES)], send_cy, 1))
 
     wait_y(0)
     top8, bottom8 = row8 == 0, row8 == HALO - 1
@@ -371,9 +414,6 @@
         weight = jnp.sum(rowk[0] * t, axis=0, keepdims=True)
         lines = jnp.where(row8 == 2 * side, moved, jnp.where(row8 == 2 * side + 1, weight, lines))
         y_faces.append((side, g, here, t, moved, weight))
-    vsend[...] = lines
-    for dx in (-1, 1):
-        start(to_all(0, dx, vsend, cxrecv.at[(1 - dx) // 2, iz, nstrips], send_cx, 4))
     wait_x(0)
     flux, weights, faces, outside = [], [], [], []
     for t in range(xtiles):
@@ -384,30 +424,19 @@
         faces.append(face)
         outside.append(there[0])
 
-    def side_sums(g):
-        low = (g % per) * 2 * nz
+    def sums_of(flux, weights, low):
         block = jnp.logical_and(lane8 >= low, lane8 < low + 2 * nz)
         sums = []
         for values in (flux, weights):
             for parity in (even8, jnp.logical_not(even8)):
-                chosen = jnp.where(jnp.logical_and(block, parity), values[g // per], 0.0)
-                sums.append(jnp.sum(chosen, axis=1, keepdims=True))
+                sums.append(jnp.sum(jnp.where(jnp.logical_and(block, parity), values, 0.0), axis=1, keepdims=True))
         return sums
+
+    def lanes_of(g):
+        return (g % per) * 2 * nz
 
     def at_sides(left, right):
         return jnp.where(first8, left, jnp.where(last8, right, 0.0))
-
-    sums = {}
-    for side, g in ((0, 0), (1, groups - 1)):
-        if g not in sums:
-            sums[g] = side_sums(g)
-        flux_l, flux_r, weight_l, weight_r = sums[g]
-        tile = nil8
-        for i, column in enumerate((-flux_r, -flux_l, weight_r, weight_l, flux_l, flux_r, weight_l, weight_r)):
-            tile = jnp.where(lane8 == i, column, tile)
-        lsend[side] = tile
-    for dy in (-1, 1):
-        start(to_all(dy, 0, lsend.at[(1 + dy) // 2], cyrecv.at[(1 - dy) // 2, iz, PLANES], send_cy, 5))
 
     for side, g, here, t, moved, weight in y_faces:
         for p, change in ((0, -moved), (1, weight), (2, weight))[:3 if side else 2]:
@@ -416,13 +445,10 @@
             edge_row = HALO - 1 + side * ny
             ty[z, edge_row:edge_row + 1, :] = t[z:z + 1]
     zplanes[iz, PLANES * groups] = lines
-    in16 = lax.rem(lane8, 2 * HALO)
     for i, tiles in enumerate(packing):
         across = nil8
         for j, g in enumerate(tiles):
-            if g not in sums:
-                sums[g] = side_sums(g)
-            flux_l, flux_r, weight_l, weight_r = sums[g]
+            flux_l, flux_r, weight_l, weight_r = sums_of(flux[g // per], weights[g // per], lanes_of(g))
             for p, change in ((0, at_sides(-flux_l, -flux_r)), (1, at_sides(weight_l, weight_r)),
                               (3, jnp.where(last8, weight_r, 0.0))):
                 planes[p][g] = planes[p][g] + change
@@ -434,7 +460,7 @@
         for g in range(groups):
             zplanes[iz, p * groups + g] = planes[p][g]
     for d in range(1, ngz):
-        remote(zplanes.at[iz], zplanes.at[iz], send_cz, c_recv.at[0],
+        remote(zplanes.at[iz, 0:first_part], zplanes.at[iz, 0:first_part], send_cz, c_recv.at[0],
                {"gx": ix, "gy": iy, "gz": lax.rem(iz + d, ngz)}).start()
 
     wait_y(1)
@@ -496,21 +522,57 @@
                 qv[r, z, tile, :] = e[r][0] * inv
         return 0
 
-    def solve_two(i, carry):
-        return solve(2 * i + 1, solve(2 * i, carry))
-
-    lax.fori_loop(0, nz // 2, solve_two, 0)
-    if nz % 2:
-        solve(nz - 1, 0)
+    def solve_part(begin, end):
+        def solve_two(i, carry):
+            return solve(begin + 2 * i + 1, solve(begin + 2 * i, carry))
+
+        lax.fori_loop(0, (end - begin) // 2, solve_two, 0)
+        if (end - begin) % 2:
+            solve(end - 1, 0)
+
+    solve_part(0, nz // 2)
 
     corners = beside_y * beside_x
+    wait_many(beside_y + beside_x, [(n, zplanes.at[0, 0:2 * n]) for n in range(1, 5)], send_cx, h_recv.at[5], False)
+    wait_many(corners, ((1, cdrecv.at[0, ngz:]), (2, cdrecv.at[0:2, ngz:]), (4, cdrecv.at[:, ngz:])), send_cd, h_recv.at[6], False)
+    from_top = group8 < layers
+    ours, theirs = [], []
+    for i in range(2):
+        ours.append(jnp.where(left_part, cxrecv[0, ngz * nstrips + i], cxrecv[1, ngz * nstrips + i]))
+        theirs.append(jnp.where(from_top, jnp.where(left_part, cdrecv[0, ngz + i], cdrecv[1, ngz + i]),
+                                jnp.where(left_part, cdrecv[2, ngz + i], cdrecv[3, ngz + i])))
+    t = jnp.where(theirs[1] > 0.0, 1.0 / (ours[1] + theirs[1]), 0.0)
+    pattern = nil8
+    for k in range(layers):
+        pattern = jnp.where(lax.rem(group8, layers) == k, rowk[0, k * HALO:(k + 1) * HALO, :], pattern)
+    both = jnp.where(top8, jnp.sum(t * (ours[0] - theirs[0]), axis=0, keepdims=True),
+                     jnp.sum(t * pattern, axis=0, keepdims=True))
+    summed = both
+    for k in range(1, layers):
+        summed = summed + pltpu.roll(both, nx - 2 * HALO * k, 1)
+    upper = pltpu.roll(summed, nx - HALO, 1)
+    lower = pltpu.roll(summed, (2 * nx - 2 * HALO * layers - HALO) % nx, 1)
+    zplanes[iz, first_part] = jnp.where(row8 < 2, upper, pltpu.roll(lower, 2, 0))
+    for side, g in ends:
+        tiles = [swapped(cyrecv[side, ngz * PLANES + i]) for i in range(2)]
+        there = [jnp.where(even8, cdrecv[2 * side, ngz + 2 + i], cdrecv[2 * side + 1, ngz + 2 + i]) for i in range(2)]
+        face = jnp.where(there[1] > 0.0, 1.0 / (tiles[1] + there[1]), 0.0)
+        flux_l, flux_r, weight_l, weight_r = sums_of(face * (tiles[0] - there[0]), face * lanek[0], lanes_of(ends[1 - side][1]))
+        for n, tile in enumerate((at_sides(-flux_l, -flux_r), at_sides(weight_l, weight_r),
+                                  at_sides(flux_r, flux_l), at_sides(weight_r, weight_l))):
+            zplanes[iz, first_part + 1 + 4 * side + n] = tile
+    for d in range(1, ngz):
+        remote(zplanes.at[iz, first_part:], zplanes.at[iz, first_part:], send_cz, c_recv.at[4],
+               {"gx": ix, "gy": iy, "gz": lax.rem(iz + d, ngz)}).start()
+    solve_part(nz // 2, nz)
+
     if ngz > 1:
-        others = zplanes.at[0:ngz - 1]
+        others = zplanes.at[0:ngz - 1, 0:first_part]
         remote(others, others, send_cz, c_recv.at[0], z_device(0)).wait_recv()
-    d_cases = ((1, cdrecv.at[0]), (2, cdrecv.at[0:2]), (4, cdrecv))
-    wait_many(beside_y, ((1, cyrecv.at[0, :, 0:PLANES]), (2, cyrecv.at[:, :, 0:PLANES])), send_cy, c_recv.at[1], False)
-    wait_many(beside_x, ((1, cxrecv.at[0, :, 0:nstrips]), (2, cxrecv.at[:, :, 0:nstrips])), send_cx, c_recv.at[2], False)
-    wait_many(corners, d_cases, send_cd, c_recv.at[3], False)
+    y_early, x_early = slice(0, ngz * PLANES), slice(0, ngz * nstrips)
+    wait_many(beside_y, ((1, cyrecv.at[0, y_early]), (2, cyrecv.at[:, y_early])), send_cy, c_recv.at[1], False)
+    wait_many(beside_x, ((1, cxrecv.at[0, x_early]), (2, cxrecv.at[:, x_early])), send_cx, c_recv.at[2], False)
+    wait_many(corners, ((1, cdrecv.at[0, 0:ngz]), (2, cdrecv.at[0:2, 0:ngz]), (4, cdrecv.at[:, 0:ngz])), send_cd, c_recv.at[3], False)
 
     def gathered(part):
         total = part(0)
@@ -519,8 +581,7 @@
         return total
 
     tiles_in = groups + 2
-    left_part = in16 < HALO
-    side_tiles = [jnp.where(left_part, gathered(lambda i: cxrecv[0, i, t]), gathered(lambda i: cxrecv[1, i, t]))
+    side_tiles = [jnp.where(left_part, gathered(lambda i: cxrecv[0, i * nstrips + t]), gathered(lambda i: cxrecv[1, i * nstrips + t]))
                   + gathered(lambda i: zplanes[i, PLANES * groups + 1 + t]) for t in range(nstrips)]
     corner_tiles = [jnp.where(left_part, gathered(lambda i: cdrecv[2 * v, i]), gathered(lambda i: cdrecv[2 * v + 1, i]))
                     for v in range(2)]
@@ -538,8 +599,8 @@
 
     b = [[border_of(p, g) for g in range(-1, groups + 1)] for p in range(PLANES)]
     own_lines = gathered(lambda i: zplanes[i, PLANES * groups])
-    a = [[gathered(lambda i: cyrecv[0, i, p])] + [gathered(lambda i: zplanes[i, p * groups + g]) for g in range(groups)]
-         + [gathered(lambda i: cyrecv[1, i, p])] for p in range(PLANES)]
+    a = [[gathered(lambda i: cyrecv[0, i * PLANES + p])] + [gathered(lambda i: zplanes[i, p * groups + g]) for g in range(groups)]
+         + [gathered(lambda i: cyrecv[1, i * PLANES + p])] for p in range(PLANES)]
 
     def beyond(grid, lines):
         for side, t, here in ((0, 0, bottom8), (1, tiles_in - 1, top8)):
@@ -580,9 +641,10 @@
     for t in range(1, tiles_in - 1):
         prepare(0, t)
 
-    wait_many(beside_x, ((1, cxrecv.at[0, :, nstrips]), (2, cxrecv.at[:, :, nstrips])), send_cx, c_recv.at[4], False)
-    lines = jnp.where(on_left, gathered(lambda i: cxrecv[0, i, nstrips]),
-                      jnp.where(on_right, gathered(lambda i: cxrecv[1, i, nstrips]), 0.0))
+    if ngz > 1:
+        rest = zplanes.at[0:ngz - 1, first_part:]
+        remote(rest, rest, send_cz, c_recv.at[4], z_device(0)).wait_recv()
+    lines = jnp.where(strip8, gathered(lambda i: zplanes[i, first_part]), 0.0)
     beyond(b, lines)
     for side, t, here in ((0, 1, top8), (1, groups, bottom8)):
         moved, weight = lines[2 * side:2 * side + 1], lines[2 * side + 1:2 * side + 2]
@@ -591,11 +653,9 @@
     fill(0, 1, b[2])
     for t in range(1, tiles_in - 1):
         prepare(1, t)
-    wait_many(beside_y, ((1, cyrecv.at[0, :, PLANES]), (2, cyrecv.at[:, :, PLANES])), send_cy, c_recv.at[5], False)
     for side, t in ((0, 0), (1, tiles_in - 1)):
-        columns = gathered(lambda i: cyrecv[side, i, PLANES])
         flux_, weight_, flux_past, weight_past = (
-            jnp.where(outer8, pltpu.roll(columns, nx - 2 * n - 1, 1), 0.0) for n in range(4))
+            gathered(lambda i: zplanes[i, first_part + 1 + 4 * side + n]) for n in range(4))
         for grid, change, weight in ((a, flux_, weight_), (b, flux_past, weight_past)):
             grid[0][t] = grid[0][t] + change
             grid[1][t] = grid[1][t] + weight
@@ -629,10 +689,11 @@
         (beside_z, z_cases, send_z),
         (beside_y, ((1, cyrecv.at[0]), (2, cyrecv)), send_cy),
         (beside_x, ((1, cxrecv.at[0]), (2, cxrecv)), send_cx),
-        (corners, d_cases, send_cd),
+        (corners, ((1, cdrecv.at[0]), (2, cdrecv.at[0:2]), (4, cdrecv)), send_cd),
     ):
         wait_many(count, cases, sem, h_recv.at[0], True)
     if ngz > 1:
+        others = zplanes.at[0:ngz - 1]
         remote(others, others, send_cz, c_recv.at[0], z_device(0)).wait_send()
 
 
@@ -690,12 +751,12 @@
             vmem(2, 2, 2 * nz, nx), vmem(2, 2, 2 * nz, nx),
             vmem(2, 2, xtiles, HALO, nx), vmem(2, 2, 2, xtiles, HALO, nx), vmem(4, xtiles, HALO, nx),
             vmem(3, nz, nx), vmem(nz + 1, ny, nx), vmem(2, ey, nx),
-            vmem(ngz, PLANES * groups + 1 + strips, HALO, nx), vmem(2, PLANES, HALO, nx), vmem(strips, HALO, nx),
-            vmem(2, ngz, PLANES + 1, HALO, nx), vmem(2, ngz, strips + 1, HALO, nx), vmem(4, ngz, HALO, nx),
-            vmem(HALO, nx), vmem(2, HALO, nx), vmem(2, 2, ey + 2 * HALO, nx),
+            vmem(ngz, PLANES * groups + 1 + strips + 9, HALO, nx), vmem(2, PLANES, HALO, nx), vmem(strips, HALO, nx),
+            vmem(2, ngz * PLANES + 2, HALO, nx), vmem(2, ngz * strips + 2, HALO, nx), vmem(4, ngz + 4, HALO, nx),
+            vmem(2, HALO, nx), vmem(2, 4, HALO, nx), vmem(2, 2, ey + 2 * HALO, nx),
             pltpu.SMEM((nz,), facies.dtype), pltpu.SMEM((3, facets, 3), f32), pltpu.SMEM((3, facets, 3), f32),
             pltpu.SMEM((NCOEF, facets), f32),
-            pltpu.SemaphoreType.REGULAR, pltpu.SemaphoreType.REGULAR, dma(7), dma(5), dma(6),
+            pltpu.SemaphoreType.REGULAR((3,)), pltpu.SemaphoreType.REGULAR, dma(7), dma(7), dma(5),
         ],
         compiler_params=pltpu.CompilerParams(collective_id=0, has_side_effects=True, vmem_limit_bytes=limit),
         name="cpr_apply",

time: 12.4 us -> 11.9 us (0.960)
  Pallas kernels: 11.6 us -> 11 us
    pallas_call x1, Pallas kernels: 10.6 us -> 9.98 us  [per_device(): pl.pallas_call(functools.partial(kernel, sizes), out_shape=(vmem(3, *cell...]
where the time goes in v3:
time: 11.9 us; the launch traced here: 11.7 us
  Pallas kernels  11 us (92%)
  between operations  0.64 us (5%)
    pallas_call x1, Pallas kernels, per_device(): pl.pallas_call(functools.partial(kernel, sizes), out_shape=(vmem(3, *cell...  9.98 us
    pallas_call x1, Pallas kernels, per_device(): pl.pallas_call(functools.partial(finish_kernel, parts), out_shape=(jax.Sh...  1.05 us

profile of v3, /device:TPU:0, one launch (start us, length us, event | category | flops | bytes accessed | tf_op | source)
XLA Modules:
  0.0 11.7 jit_solution(8232791776462592213)
XLA Ops:
  0.6 10.0 %cpr_apply.1 = (f32[3,16,40,128]{3,2,1,0:T(8,128)S(1)}, f32[3,16,40,128]{3,2,1,0:T(8,128)S(1)}, f32[16,40,128]{2,1,0:T(8,128)S(1)}, f32[16,56,128]{2,1,0:T(8,128...) custom-call(s32[16]{0:T(128)} %facies_hbm.1, f32[3,4,3]{2,1,0:T(4,128)} %bitcast.2, ...), custom_call_target="tpu_custom_call" | custom-call | tf_op jit(solution)/shard_map/cpr_apply/pallas_call | solution.py:742
  10.6 1.0 %cpr_finish.1 = (f32[3,16,40,128]{3,2,1,0:T(8,128)}, f32[40,128]{1,0:T(8,128)}) custom-call(f32[3,16,40,128]{3,2,1,0:T(8,128)S(1)} %get-tuple-element.9.w, f32[3,16,40,128]{3,2,1,0:T(8,128)S(1)} %get-tuple-element.10.qv, f32[16,40,128]{2,1,0:T(8,128)S(1)} %get-tuple-element.11.tzs, f32[16,56,128]{2,1,0:T(8,128)S(1)} %get-tuple-element.12.ty, ...), custom_call_target="tpu_custom_call" | custom-call | tf_op jit(solution)/shard_map/cpr_finish/pallas_call | solution.py:766

commit v4 on v3

--- a/solution.py
+++ b/solution.py
@@ -55,8 +55,8 @@
 def kernel(sizes, facies_hbm, mtab_hbm, ktab_hbm, state_hbm, rhs_hbm, perm_hbm, pore_hbm,
            w, qv, tzs, ty, txp, txm, final,
            u, pcb, rhs, permb, poreb, ysend, yrecv, xsend, xrecv, edge, rowk, tzf, shifted,
-           zplanes, ystrips, strips, cyrecv, cxrecv, cdrecv, rpsend, dsend, field,
-           facies, mtab, ktab, ctab, near, far_sem, in_sem, h_recv, c_recv):
+           zplanes, ystrips, strips, cyrecv, cxrecv, cdrecv, rpsend, dsend, yedge, field,
+           facies, mtab, ktab, ctab, near, far, in_sem, h_recv, c_recv):
     ngx, ngy, ngz, nz, ny, nx = sizes
     ix, iy, iz = lax.axis_index("gx"), lax.axis_index("gy"), lax.axis_index("gz")
     own = slice(HALO, HALO + ny)
@@ -67,6 +67,8 @@
     layers = nz // HALO
     ends = ((0, 0), (1, groups - 1))
     first_part = PLANES * groups + 1 + nstrips
+    raw_lane = nx - 4 * HALO * layers
+    assert nz % HALO == 0 and raw_lane >= 2 * nz
     f32 = jnp.float32
     send_y, send_x, send_z, send_cy, send_cx, send_cd, send_cz = (in_sem.at[i] for i in (0, 1, 4, 5, 6, 2, 3))
 
@@ -128,6 +130,10 @@
     zero(field)
     for z in range(nz):
         zero(pcb.at[z, HALO + ny:])
+        zero(ty.at[z, 0:HALO])
+        for k in range(3):
+            zero(u.at[k, z + 1, 0:HALO])
+            zero(u.at[k, z + 1, HALO + ny:])
     zero(shifted.at[:, 0:HALO])
 
     for i in (4, 6, 5):
@@ -215,10 +221,10 @@
     start(y_copies(0))
     start(x_copies(0))
     start([(has_above, z_up), (has_below, z_down)])
-    for n, dy in ((1, -1), (0, 1)):
-        @pl.when(exists(dy, 0))
-        def _(n=n, dy=dy):
-            pl.semaphore_signal(near.at[n], inc=1, device_id=at(dy, 0), device_id_type=MESH)
+    for n, dy, dx in ((1, -1, 0), (0, 1, 0), (3, 0, 1)):
+        @pl.when(exists(dy, dx))
+        def _(n=n, dy=dy, dx=dx):
+            pl.semaphore_signal(near.at[n], inc=1, device_id=at(dy, dx), device_id_type=MESH)
     signal_peers(near.at[2])
 
     def counted(count, cases, descriptor, done):
@@ -252,6 +258,11 @@
             xsend[1, i, t] = packed[t]
     start(x_copies(1))
     start(y_copies(1))
+    raw_group8 = group8 - raw_lane // (2 * HALO)
+
+    def lanes_of(g):
+        return (g % per) * 2 * nz
+
     for i in range(2):
         here, swap = nil8, nil8
         for side in range(2):
@@ -259,15 +270,17 @@
                 rows = slice(i * nz + k * HALO, i * nz + (k + 1) * HALO)
                 for other in range(2):
                     slot = (side if not other else 1 - side) * layers + k
-                    moved = pltpu.roll(ysend[0, side, rows, :], (2 * HALO * slot + HALO) % nx, 1)
+                    moved = pltpu.roll(ysend[0, side, rows, :], (raw_lane + 2 * HALO * slot + HALO) % nx, 1)
                     if other:
-                        swap = jnp.where(group8 == slot, moved, swap)
+                        swap = jnp.where(raw_group8 == slot, moved, swap)
                     else:
-                        here = jnp.where(group8 == slot, moved, here)
+                        here = jnp.where(raw_group8 == slot, moved, here)
         rpsend[i] = here
         for side, g in ends:
-            dsend[side, i] = swap
-            dsend[side, 2 + i] = xsend[0, i, g // per]
+            column = xsend[0, i, g // per]
+            if lanes_of(g):
+                column = pltpu.roll(column, nx - lanes_of(g), 1)
+            dsend[side, i] = jnp.where(lane8 < 2 * nz, column, swap)
 
     def ways(dy, dx, copy):
         @pl.when(exists(dy, dx))
@@ -277,15 +290,15 @@
     for dx in (-1, 1):
         ways(0, dx, remote(rpsend, cxrecv.at[(1 - dx) // 2, ngz * nstrips:], send_cx, h_recv.at[5], at(0, dx)))
     for dy in (-1, 1):
-        ways(dy, 0, remote(dsend.at[(1 + dy) // 2, 2:], cyrecv.at[(1 - dy) // 2, ngz * PLANES:], send_cy, h_recv.at[5], at(dy, 0)))
-
-    def raw_corners(dy):
-        @pl.when(exists(dy, 0))
+        ways(dy, 0, remote(dsend.at[(1 + dy) // 2], cyrecv.at[(1 - dy) // 2, ngz * PLANES:], send_cy, h_recv.at[5], at(dy, 0)))
+
+    def known(n, dy, dx):
+        @pl.when(exists(dy, dx))
         def _():
-            pl.semaphore_wait(near.at[(1 + dy) // 2], 1)
-        for dx in (-1, 1):
-            ways(dy, dx, remote(dsend.at[(1 + dy) // 2], cdrecv.at[(1 - dy) + (1 - dx) // 2, ngz:], send_cd, h_recv.at[6],
-                                at(dy, dx)))
+            pl.semaphore_wait(near.at[n], 1)
+
+    def raw_corner(dy, dx):
+        ways(dy, dx, remote(dsend.at[(1 + dy) // 2], cdrecv.at[(1 - dy) + (1 - dx) // 2, ngz:], send_cd, h_recv.at[6], at(dy, dx)))
 
 
     layer_of_lane = lax.rem(lane8[0:1], 2 * nz) // 2
@@ -298,13 +311,10 @@
     loads[2].wait()
     loads[3].wait()
 
-    raw_corners(-1)
-
-    for f in range(ktab.shape[1]):
-        values = block_scalars([[mtab[r, f, c] for c in range(3)] for r in range(3)],
-                               [[ktab[r, f, c] for c in range(3)] for r in range(3)])
-        for i, value in enumerate(values):
-            ctab[i, f] = value
+    known(0, -1, 0)
+    raw_corner(-1, -1)
+    raw_corner(-1, 1)
+    signal_peers(far.at[0])
 
     def tile_of(g):
         return slice(g * HALO, (g + 1) * HALO)
@@ -374,9 +384,6 @@
             d = [u[k, inside, rows, :] - u[k, slot, rows, :] for k in range(3)]
             p_rhs[g] = p_rhs[g] - t * (k0[0] * d[0] + k0[1] * d[1] + k0[2] * d[2])
     mine = [[swapped(xsend[0, i, t]) for t in range(xtiles)] for i in range(2)]
-    raw_corners(1)
-    pl.semaphore_wait(near.at[2], ngz - 1)
-    signal_peers(far_sem)
 
     planes = [p_rhs, p_dia, s_ty, s_tx]
     for p in range(PLANES):
@@ -390,18 +397,72 @@
                 strip = jnp.where(group8 == slot, pltpu.roll(planes[p][g], (2 * HALO * slot + HALO) % nx, 1), strip)
         strips[i] = strip
 
-    pl.semaphore_wait(far_sem, ngz - 1)
-
-    def to_all(dy, dx, src, dst, send, recv):
+    def to_all(dy, dx, src, dst, send, recv, parts=range(ngz)):
         return [(exists(dy, dx), remote(src, dst, send, c_recv.at[recv],
-                                        {"gx": ix + dx, "gy": iy + dy, "gz": lax.rem(iz + d, ngz)})) for d in range(ngz)]
-
-    for dy, dx in SIDES[4:]:
-        start(to_all(dy, dx, strips.at[0 if dy < 0 else last_head], cdrecv.at[(1 - dy) + (1 - dx) // 2, iz], send_cd, 3))
+                                        {"gx": ix + dx, "gy": iy + dy, "gz": lax.rem(iz + d, ngz)})) for d in parts]
+
+    def corner_strips(dy, dx, parts):
+        start(to_all(dy, dx, strips.at[0 if dy < 0 else last_head], cdrecv.at[(1 - dy) + (1 - dx) // 2, iz], send_cd, 3, parts))
+
+    pl.semaphore_wait(far.at[0], ngz - 1)
+    pl.semaphore_wait(near.at[2], ngz - 1)
+    corner_strips(-1, -1, range(ngz))
+    corner_strips(-1, 1, range(ngz))
+    known(3, 0, -1)
+    raw_corner(1, -1)
+    corner_strips(1, -1, range(1))
     for dx in (-1, 1):
         start(to_all(0, dx, strips, cxrecv.at[(1 - dx) // 2, pl.ds(iz * nstrips, nstrips)], send_cx, 2))
     for dy in (-1, 1):
         start(to_all(dy, 0, ystrips.at[(1 + dy) // 2], cyrecv.at[(1 - dy) // 2, pl.ds(iz * PLANES, PLANES)], send_cy, 1))
+
+    for f in range(ktab.shape[1]):
+        values = block_scalars([[mtab[r, f, c] for c in range(3)] for r in range(3)],
+                               [[ktab[r, f, c] for c in range(3)] for r in range(3)])
+        for i, value in enumerate(values):
+            ctab[i, f] = value
+
+    known(1, 1, 0)
+    raw_corner(1, 1)
+    signal_peers(far.at[1])
+    corner_strips(1, 1, range(1))
+
+    def inside(z, _):
+        f = facies[z]
+        kinv = [[ctab[KINV + 3 * r + c, f] for c in range(3)] for r in range(3)]
+        for g in range(groups):
+            rows = padded(g, 0)
+            tile = tile_of(g)
+            tzm, tzp = tzf[z, tile, :], tzf[z + 1, tile, :]
+            typ, tym = ty[z, rows, :], ty[z, padded(g, -1), :]
+            xp = txp[z, tile, :]
+            xm = pltpu.roll(xp, 1, 1)
+            tz = tzm + tzp
+            tzs[z, tile, :] = tz
+            txm[z, tile, :] = xm
+            qv[0, z, tile, :] = tz + (typ + tym) + (xp + xm)
+            given = [rhs[k, z, tile, :] for k in range(3)]
+            for k in range(3):
+                c = u[k, z + 1, rows, :]
+                w[k, z, tile, :] = ((tzp * u[k, z + 2, rows, :] + tzm * u[k, z, rows, :])
+                                    + (typ * u[k, z + 1, padded(g, 1), :] + tym * u[k, z + 1, padded(g, -1), :])
+                                    + (xp * pltpu.roll(c, nx - 1, 1) + xm * pltpu.roll(c, 1, 1))
+                                    + (kinv[k][0] * given[0] + kinv[k][1] * given[1] + kinv[k][2] * given[2]))
+        return 0
+
+    def layers_of(step, begin, end):
+        def several(i, carry):
+            return step(begin + 2 * i + 1, step(begin + 2 * i, carry))
+
+        lax.fori_loop(0, (end - begin) // 2, several, 0)
+        if (end - begin) % 2:
+            step(end - 1, 0)
+
+    layers_of(inside, 0, nz // 2)
+    pl.semaphore_wait(far.at[1], ngz - 1)
+    corner_strips(1, -1, range(1, ngz))
+    corner_strips(1, 1, range(1, ngz))
+    layers_of(inside, nz // 2, nz)
 
     wait_y(0)
     top8, bottom8 = row8 == 0, row8 == HALO - 1
@@ -431,9 +492,6 @@
             for parity in (even8, jnp.logical_not(even8)):
                 sums.append(jnp.sum(jnp.where(jnp.logical_and(block, parity), values, 0.0), axis=1, keepdims=True))
         return sums
-
-    def lanes_of(g):
-        return (g % per) * 2 * nz
 
     def at_sides(left, right):
         return jnp.where(first8, left, jnp.where(last8, right, 0.0))
@@ -466,12 +524,12 @@
     wait_y(1)
     wait_x(1)
     invrow = 1.0 / rowk[0]
-    for side, at_row in ((0, HALO - 1), (1, HALO + ny)):
+    for side, _, _, t, _, _ in y_faces:
         one, two_ = yrecv[1, side, :nz, :], yrecv[1, side, nz:, :]
         zero_ = (yrecv[0, side, :nz, :] - rowk[1] * one - rowk[2] * two_) * invrow
-        for z in range(nz):
-            for k, x in enumerate((zero_, one, two_)):
-                u[k, z + 1, at_row:at_row + 1, :] = x[z:z + 1]
+        for k, x in enumerate((zero_, one, two_)):
+            yedge[side, k] = t * x
+        yedge[side, 3] = t
     invlane = 1.0 / lanek[0]
     for t in range(xtiles):
         one, two_ = (jnp.where(even8, xrecv[1, 0, i, t], xrecv[1, 1, i, t]) for i in range(2))
@@ -485,35 +543,23 @@
     def solve(z, _):
         volume = poreb[z].astype(f32)
         f = facies[z]
-        kinv = [[ctab[KINV + 3 * r + c, f] for c in range(3)] for r in range(3)]
         n = [[ctab[NMAT + 3 * r + c, f] for c in range(3)] for r in range(3)]
         adj = [[ctab[NADJ + 3 * r + c, f] for c in range(3)] for r in range(3)]
         dia = [ctab[NDIA + i, f] for i in range(3)]
         trace, minors, det_n = ctab[NTR, f], ctab[NC2, f], ctab[NDET, f]
         for g in range(groups):
-            rows = padded(g, 0)
             tile = tile_of(g)
-            shift = lax.rem(2 * nx - (2 * nz * (g % per) + 1) - 2 * z, nx)
-            lateral = [jnp.where(outer8, pltpu.roll(edge[k, g // per], shift, 1), 0.0) for k in range(4)]
-            tzm, tzp = tzf[z, tile, :], tzf[z + 1, tile, :]
-            typ, tym = ty[z, rows, :], ty[z, padded(g, -1), :]
-            xp = txp[z, tile, :]
-            xm = pltpu.roll(xp, 1, 1)
-            tz = tzm + tzp
-            tzs[z, tile, :] = tz
-            total = tz + (typ + tym) + (xp + xm) + lateral[3]
-            txp[z, tile, :] = xp + jnp.where(last8, lateral[3], 0.0)
-            txm[z, tile, :] = xm + jnp.where(first8, lateral[3], 0.0)
-            near = []
-            for k in range(3):
-                c = u[k, z + 1, rows, :]
-                near.append(tzp * u[k, z + 2, rows, :] + tzm * u[k, z, rows, :]
-                            + typ * u[k, z + 1, padded(g, 1), :] + tym * u[k, z + 1, padded(g, -1), :]
-                            + xp * pltpu.roll(c, nx - 1, 1) + xm * pltpu.roll(c, 1, 1) + lateral[k])
-            given = [rhs[k, z, tile, :] for k in range(3)]
-            b = [near[r] + kinv[r][0] * given[0] + kinv[r][1] * given[1] + kinv[r][2] * given[2] for r in range(3)]
+            shift = lax.rem(2 * nx - (lanes_of(g) + 1) - 2 * z, nx)
+            added = [jnp.where(outer8, pltpu.roll(edge[k, g // per], shift, 1), 0.0) for k in range(4)]
+            txp[z, tile, :] = txp[z, tile, :] + jnp.where(last8, added[3], 0.0)
+            txm[z, tile, :] = txm[z, tile, :] + jnp.where(first8, added[3], 0.0)
+            for side, head in ends:
+                if g == head:
+                    here = top8 if side == 0 else bottom8
+                    added = [added[k] + jnp.where(here, yedge[side, k, pl.ds(z, 1), :], 0.0) for k in range(4)]
+            b = [w[r, z, tile, :] + added[r] for r in range(3)]
             v = volume[tile]
-            s = total * (1.0 / v)
+            s = (qv[0, z, tile, :] + added[3]) * (1.0 / v)
             e = [[s * (s + dia[r]) + adj[r][r] if r == c else adj[r][c] - s * n[r][c] for c in range(3)] for r in range(3)]
             det = ((s + trace) * s + minors) * s + det_n
             inv = 1.0 / (v * det)
@@ -522,49 +568,42 @@
                 qv[r, z, tile, :] = e[r][0] * inv
         return 0
 
-    def solve_part(begin, end):
-        def solve_two(i, carry):
-            return solve(begin + 2 * i + 1, solve(begin + 2 * i, carry))
-
-        lax.fori_loop(0, (end - begin) // 2, solve_two, 0)
-        if (end - begin) % 2:
-            solve(end - 1, 0)
-
-    solve_part(0, nz // 2)
+    most = nz * 5 // 8
+    layers_of(solve, 0, most)
 
     corners = beside_y * beside_x
     wait_many(beside_y + beside_x, [(n, zplanes.at[0, 0:2 * n]) for n in range(1, 5)], send_cx, h_recv.at[5], False)
     wait_many(corners, ((1, cdrecv.at[0, ngz:]), (2, cdrecv.at[0:2, ngz:]), (4, cdrecv.at[:, ngz:])), send_cd, h_recv.at[6], False)
-    from_top = group8 < layers
+    from_top = raw_group8 < layers
     ours, theirs = [], []
     for i in range(2):
         ours.append(jnp.where(left_part, cxrecv[0, ngz * nstrips + i], cxrecv[1, ngz * nstrips + i]))
         theirs.append(jnp.where(from_top, jnp.where(left_part, cdrecv[0, ngz + i], cdrecv[1, ngz + i]),
                                 jnp.where(left_part, cdrecv[2, ngz + i], cdrecv[3, ngz + i])))
-    t = jnp.where(theirs[1] > 0.0, 1.0 / (ours[1] + theirs[1]), 0.0)
+    t = jnp.where(jnp.logical_and(raw_group8 >= 0, theirs[1] > 0.0), 1.0 / (ours[1] + theirs[1]), 0.0)
     pattern = nil8
     for k in range(layers):
-        pattern = jnp.where(lax.rem(group8, layers) == k, rowk[0, k * HALO:(k + 1) * HALO, :], pattern)
+        pattern = jnp.where(lax.rem(group8, layers) == (k + raw_lane // (2 * HALO)) % layers, rowk[0, k * HALO:(k + 1) * HALO, :], pattern)
     both = jnp.where(top8, jnp.sum(t * (ours[0] - theirs[0]), axis=0, keepdims=True),
                      jnp.sum(t * pattern, axis=0, keepdims=True))
     summed = both
     for k in range(1, layers):
         summed = summed + pltpu.roll(both, nx - 2 * HALO * k, 1)
-    upper = pltpu.roll(summed, nx - HALO, 1)
-    lower = pltpu.roll(summed, (2 * nx - 2 * HALO * layers - HALO) % nx, 1)
+    upper = pltpu.roll(summed, (2 * nx - raw_lane - HALO) % nx, 1)
+    lower = pltpu.roll(summed, (2 * nx - raw_lane - 2 * HALO * layers - HALO) % nx, 1)
     zplanes[iz, first_part] = jnp.where(row8 < 2, upper, pltpu.roll(lower, 2, 0))
     for side, g in ends:
         tiles = [swapped(cyrecv[side, ngz * PLANES + i]) for i in range(2)]
-        there = [jnp.where(even8, cdrecv[2 * side, ngz + 2 + i], cdrecv[2 * side + 1, ngz + 2 + i]) for i in range(2)]
+        there = [jnp.where(even8, cdrecv[2 * side, ngz + i], cdrecv[2 * side + 1, ngz + i]) for i in range(2)]
         face = jnp.where(there[1] > 0.0, 1.0 / (tiles[1] + there[1]), 0.0)
-        flux_l, flux_r, weight_l, weight_r = sums_of(face * (tiles[0] - there[0]), face * lanek[0], lanes_of(ends[1 - side][1]))
+        flux_l, flux_r, weight_l, weight_r = sums_of(face * (tiles[0] - there[0]), face * lanek[0], 0)
         for n, tile in enumerate((at_sides(-flux_l, -flux_r), at_sides(weight_l, weight_r),
                                   at_sides(flux_r, flux_l), at_sides(weight_r, weight_l))):
             zplanes[iz, first_part + 1 + 4 * side + n] = tile
     for d in range(1, ngz):
         remote(zplanes.at[iz, first_part:], zplanes.at[iz, first_part:], send_cz, c_recv.at[4],
                {"gx": ix, "gy": iy, "gz": lax.rem(iz + d, ngz)}).start()
-    solve_part(nz // 2, nz)
+    layers_of(solve, most, nz)
 
     if ngz > 1:
         others = zplanes.at[0:ngz - 1, 0:first_part]
@@ -752,11 +791,11 @@
             vmem(2, 2, xtiles, HALO, nx), vmem(2, 2, 2, xtiles, HALO, nx), vmem(4, xtiles, HALO, nx),
             vmem(3, nz, nx), vmem(nz + 1, ny, nx), vmem(2, ey, nx),
             vmem(ngz, PLANES * groups + 1 + strips + 9, HALO, nx), vmem(2, PLANES, HALO, nx), vmem(strips, HALO, nx),
-            vmem(2, ngz * PLANES + 2, HALO, nx), vmem(2, ngz * strips + 2, HALO, nx), vmem(4, ngz + 4, HALO, nx),
-            vmem(2, HALO, nx), vmem(2, 4, HALO, nx), vmem(2, 2, ey + 2 * HALO, nx),
+            vmem(2, ngz * PLANES + 2, HALO, nx), vmem(2, ngz * strips + 2, HALO, nx), vmem(4, ngz + 2, HALO, nx),
+            vmem(2, HALO, nx), vmem(2, 2, HALO, nx), vmem(2, 4, nz, nx), vmem(2, 2, ey + 2 * HALO, nx),
             pltpu.SMEM((nz,), facies.dtype), pltpu.SMEM((3, facets, 3), f32), pltpu.SMEM((3, facets, 3), f32),
             pltpu.SMEM((NCOEF, facets), f32),
-            pltpu.SemaphoreType.REGULAR((3,)), pltpu.SemaphoreType.REGULAR, dma(7), dma(7), dma(5),
+            pltpu.SemaphoreType.REGULAR((4,)), pltpu.SemaphoreType.REGULAR((2,)), dma(7), dma(7), dma(5),
         ],
         compiler_params=pltpu.CompilerParams(collective_id=0, has_side_effects=True, vmem_limit_bytes=limit),
         name="cpr_apply",

time: 11.9 us -> 11.5 us (0.966)
  Pallas kernels: 11 us -> 10.7 us
    pallas_call x1, Pallas kernels: 9.98 us -> 9.62 us  [per_device(): pl.pallas_call(functools.partial(kernel, sizes), out_shape=(vmem(3, *cell...]
where the time goes in v4:
time: 11.5 us; the launch traced here: 11.3 us
  Pallas kernels  10.7 us (93%)
  between operations  0.64 us (6%)
    pallas_call x1, Pallas kernels, per_device(): pl.pallas_call(functools.partial(kernel, sizes), out_shape=(vmem(3, *cell...  9.62 us
    pallas_call x1, Pallas kernels, per_device(): pl.pallas_call(functools.partial(finish_kernel, parts), out_shape=(jax.Sh...  1.05 us

profile of v4, /device:TPU:0, one launch (start us, length us, event | category | flops | bytes accessed | tf_op | source)
XLA Modules:
  0.0 11.3 jit_solution(14739461887137739706)
XLA Ops:
  0.6 9.6 %cpr_apply.1 = (f32[3,16,40,128]{3,2,1,0:T(8,128)S(1)}, f32[3,16,40,128]{3,2,1,0:T(8,128)S(1)}, f32[16,40,128]{2,1,0:T(8,128)S(1)}, f32[16,56,128]{2,1,0:T(8,128...) custom-call(s32[16]{0:T(128)} %facies_hbm.1, f32[3,4,3]{2,1,0:T(4,128)} %bitcast.2, ...), custom_call_target="tpu_custom_call" | custom-call | tf_op jit(solution)/shard_map/cpr_apply/pallas_call | solution.py:781
  10.3 1.0 %cpr_finish.1 = (f32[3,16,40,128]{3,2,1,0:T(8,128)}, f32[40,128]{1,0:T(8,128)}) custom-call(f32[3,16,40,128]{3,2,1,0:T(8,128)S(1)} %get-tuple-element.9.w, f32[3,16,40,128]{3,2,1,0:T(8,128)S(1)} %get-tuple-element.10.qv, f32[16,40,128]{2,1,0:T(8,128)S(1)} %get-tuple-element.11.tzs, f32[16,56,128]{2,1,0:T(8,128)S(1)} %get-tuple-element.12.ty, ...), custom_call_target="tpu_custom_call" | custom-call | tf_op jit(solution)/shard_map/cpr_finish/pallas_call | solution.py:805

commit v5 on v4

--- a/solution.py
+++ b/solution.py
@@ -322,48 +322,37 @@
     def padded(g, shift):
         return slice(HALO + g * HALO + shift, HALO + (g + 1) * HALO + shift)
 
-    def assemble(z, carry, upper=True):
-        s_res, s_dia, s_ty, s_tx, s_hx, s_hy, s_z = (list(c) for c in carry)
-        volume = poreb[z].astype(f32)
-        k00 = coefficient(ktab, z, 0, 0)
-        m0 = [coefficient(mtab, z, 0, k) for k in range(3)]
-        if upper:
-            dk = [coefficient(ktab, z, 0, k) - coefficient(ktab, z + 1, 0, k) for k in range(3)]
-        for g in range(groups):
-            rows = padded(g, 0)
+    def assemble(g):
+        rows, tile = padded(g, 0), tile_of(g)
+        res, dia, s_y, s_x, h_x, h_y, h_z = (nil8,) * 7
+        for z in range(nz):
+            v = poreb[z].astype(f32)[tile]
+            k00 = coefficient(ktab, z, 0, 0)
+            m0 = [coefficient(mtab, z, 0, k) for k in range(3)]
             r = u[3, z + 1, rows, :]
             typ = 1.0 / (r + u[3, z + 1, padded(g, 1), :])
             if g == groups - 1:
                 typ = jnp.where(row8 < HALO - 1, typ, 0.0)
             xp = jnp.where(last8, 0.0, 1.0 / (r + pltpu.roll(r, nx - 1, 1)))
             ty[z, rows, :] = typ
-            txp[z, tile_of(g), :] = xp
+            txp[z, tile, :] = xp
             pc = pcb[z, rows, :]
-            s_hx[g] = s_hx[g] + xp * (pc - pltpu.roll(pc, nx - 1, 1))
-            s_hy[g] = s_hy[g] + typ * (pc - pcb[z, padded(g, 1), :])
-            v = volume[tile_of(g)]
+            h_x = h_x + xp * (pc - pltpu.roll(pc, nx - 1, 1))
+            h_y = h_y + typ * (pc - pcb[z, padded(g, 1), :])
             c = [u[k, z + 1, rows, :] for k in range(3)]
-            s_res[g] = s_res[g] + (rhs[0, z, tile_of(g), :] - v * (m0[0] * c[0] + m0[1] * c[1] + m0[2] * c[2]))
-            s_dia[g] = s_dia[g] + v * m0[0]
-            s_ty[g] = s_ty[g] + k00 * typ
-            s_tx[g] = s_tx[g] + k00 * xp
-            if upper:
+            res = res + (rhs[0, z, tile, :] - v * (m0[0] * c[0] + m0[1] * c[1] + m0[2] * c[2]))
+            dia = dia + v * m0[0]
+            s_y = s_y + k00 * typ
+            s_x = s_x + k00 * xp
+            if z < nz - 1:
+                dk = [coefficient(ktab, z, 0, k) - coefficient(ktab, z + 1, 0, k) for k in range(3)]
                 t = 1.0 / (r + u[3, z + 2, rows, :])
-                tzf[z + 1, tile_of(g), :] = t
+                tzf[z + 1, tile, :] = t
                 d = [c[k] - u[k, z + 2, rows, :] for k in range(3)]
-                s_z[g] = s_z[g] + t * (dk[0] * d[0] + dk[1] * d[1] + dk[2] * d[2])
-        return tuple(tuple(s) for s in (s_res, s_dia, s_ty, s_tx, s_hx, s_hy, s_z))
-
-    carry = ((nil8,) * groups,) * 7
-    trips = (nz - 1) // 2
-
-    def two(i, carry):
-        return assemble(2 * i + 1, assemble(2 * i, carry))
-
-    carry = lax.fori_loop(0, trips, two, carry)
-    for z in range(2 * trips, nz):
-        carry = assemble(z, carry, upper=z < nz - 1)
-    s_res, s_dia, s_ty, s_tx, s_hx, s_hy, s_z = (list(c) for c in carry)
+                h_z = h_z + t * (dk[0] * d[0] + dk[1] * d[1] + dk[2] * d[2])
+        return res, dia, s_y, s_x, h_x, h_y, h_z
+
+    s_res, s_dia, s_ty, s_tx, s_hx, s_hy, s_z = (list(c) for c in zip(*(assemble(g) for g in range(groups))))
 
     for g in range(groups):
         shifted[0, padded(g, 0), :] = s_hy[g]
@@ -451,12 +440,8 @@
         return 0
 
     def layers_of(step, begin, end):
-        def several(i, carry):
-            return step(begin + 2 * i + 1, step(begin + 2 * i, carry))
-
-        lax.fori_loop(0, (end - begin) // 2, several, 0)
-        if (end - begin) % 2:
-            step(end - 1, 0)
+        for z in range(begin, end):
+            step(z, 0)
 
     layers_of(inside, 0, nz // 2)
     pl.semaphore_wait(far.at[1], ngz - 1)
@@ -549,14 +534,14 @@
         trace, minors, det_n = ctab[NTR, f], ctab[NC2, f], ctab[NDET, f]
         for g in range(groups):
             tile = tile_of(g)
-            shift = lax.rem(2 * nx - (lanes_of(g) + 1) - 2 * z, nx)
+            shift = (2 * nx - (lanes_of(g) + 1) - 2 * z) % nx
             added = [jnp.where(outer8, pltpu.roll(edge[k, g // per], shift, 1), 0.0) for k in range(4)]
             txp[z, tile, :] = txp[z, tile, :] + jnp.where(last8, added[3], 0.0)
             txm[z, tile, :] = txm[z, tile, :] + jnp.where(first8, added[3], 0.0)
             for side, head in ends:
                 if g == head:
                     here = top8 if side == 0 else bottom8
-                    added = [added[k] + jnp.where(here, yedge[side, k, pl.ds(z, 1), :], 0.0) for k in range(4)]
+                    added = [added[k] + jnp.where(here, yedge[side, k, z:z + 1, :], 0.0) for k in range(4)]
             b = [w[r, z, tile, :] + added[r] for r in range(3)]
             v = volume[tile]
             s = (qv[0, z, tile, :] + added[3]) * (1.0 / v)

time: 11.5 us -> 11.4 us (level)
  the two profiles are of different devices: /device:TPU:0 before, /device:TPU:1 now
where the time goes in v5:
time: 11.4 us; the launch traced here: 11.3 us
  Pallas kernels  10.6 us (93%)
  between operations  0.64 us (6%)
    pallas_call x1, Pallas kernels, per_device(): pl.pallas_call(functools.partial(kernel, sizes), out_shape=(vmem(3, *cell...  9.57 us
    pallas_call x1, Pallas kernels, per_device(): pl.pallas_call(functools.partial(finish_kernel, parts), out_shape=(jax.Sh...  1.05 us

profile of v5, /device:TPU:1, one launch (start us, length us, event | category | flops | bytes accessed | tf_op | source)
XLA Modules:
  0.0 11.3 jit_solution(4141078848796507996)
XLA Ops:
  0.6 9.6 %cpr_apply.1 = (f32[3,16,40,128]{3,2,1,0:T(8,128)S(1)}, f32[3,16,40,128]{3,2,1,0:T(8,128)S(1)}, f32[16,40,128]{2,1,0:T(8,128)S(1)}, f32[16,56,128]{2,1,0:T(8,128...) custom-call(s32[16]{0:T(128)} %facies_hbm.1, f32[3,4,3]{2,1,0:T(4,128)} %bitcast.2, ...), custom_call_target="tpu_custom_call" | custom-call | tf_op jit(solution)/shard_map/cpr_apply/pallas_call | solution.py:766
  10.2 1.0 %cpr_finish.1 = (f32[3,16,40,128]{3,2,1,0:T(8,128)}, f32[40,128]{1,0:T(8,128)}) custom-call(f32[3,16,40,128]{3,2,1,0:T(8,128)S(1)} %get-tuple-element.9.w, f32[3,16,40,128]{3,2,1,0:T(8,128)S(1)} %get-tuple-element.10.qv, f32[16,40,128]{2,1,0:T(8,128)S(1)} %get-tuple-element.11.tzs, f32[16,56,128]{2,1,0:T(8,128)S(1)} %get-tuple-element.12.ty, ...), custom_call_target="tpu_custom_call" | custom-call | tf_op jit(solution)/shard_map/cpr_finish/pallas_call | solution.py:790

commit v6 on v5

--- a/solution.py
+++ b/solution.py
@@ -55,7 +55,7 @@
 def kernel(sizes, facies_hbm, mtab_hbm, ktab_hbm, state_hbm, rhs_hbm, perm_hbm, pore_hbm,
            w, qv, tzs, ty, txp, txm, final,
            u, pcb, rhs, permb, poreb, ysend, yrecv, xsend, xrecv, edge, rowk, tzf, shifted,
-           zplanes, ystrips, strips, cyrecv, cxrecv, cdrecv, rpsend, dsend, yedge, field,
+           zplanes, ystrips, strips, cyrecv, cxrecv, cdrecv, rpsend, dsend, swsend, yedge, field,
            facies, mtab, ktab, ctab, near, far, in_sem, h_recv, c_recv):
     ngx, ngy, ngz, nz, ny, nx = sizes
     ix, iy, iz = lax.axis_index("gx"), lax.axis_index("gy"), lax.axis_index("gz")
@@ -218,14 +218,22 @@
     z_down = remote(u.at[:, 1, own], u.at[:, nz + 1, own], send_z, h_recv.at[0], z_device(-1))
     has_below, has_above = iz > 0, iz < ngz - 1
 
+    for n, dy, dx in ((1, -1, 0), (0, 1, 0), (2, 0, 1)):
+        @pl.when(exists(dy, dx))
+        def _(n=n, dy=dy, dx=dx):
+            pl.semaphore_signal(near.at[n], inc=1, device_id=at(dy, dx), device_id_type=MESH)
     start(y_copies(0))
     start(x_copies(0))
     start([(has_above, z_up), (has_below, z_down)])
-    for n, dy, dx in ((1, -1, 0), (0, 1, 0), (3, 0, 1)):
-        @pl.when(exists(dy, dx))
-        def _(n=n, dy=dy, dx=dx):
-            pl.semaphore_signal(near.at[n], inc=1, device_id=at(dy, dx), device_id_type=MESH)
-    signal_peers(near.at[2])
+
+    def around(tiles, per_part):
+        cases = []
+        for cy in range(3):
+            for cx in range(3):
+                n = tiles(cy, cx)
+                if n:
+                    cases.append((3 * cy + cx, zplanes.at[:, 0:n] if per_part else zplanes.at[0, 0:n]))
+        return cases
 
     def counted(count, cases, descriptor, done):
         for n, ref in cases:
@@ -289,8 +297,6 @@
 
     for dx in (-1, 1):
         ways(0, dx, remote(rpsend, cxrecv.at[(1 - dx) // 2, ngz * nstrips:], send_cx, h_recv.at[5], at(0, dx)))
-    for dy in (-1, 1):
-        ways(dy, 0, remote(dsend.at[(1 + dy) // 2], cyrecv.at[(1 - dy) // 2, ngz * PLANES:], send_cy, h_recv.at[5], at(dy, 0)))
 
     def known(n, dy, dx):
         @pl.when(exists(dy, dx))
@@ -298,7 +304,7 @@
             pl.semaphore_wait(near.at[n], 1)
 
     def raw_corner(dy, dx):
-        ways(dy, dx, remote(dsend.at[(1 + dy) // 2], cdrecv.at[(1 - dy) + (1 - dx) // 2, ngz:], send_cd, h_recv.at[6], at(dy, dx)))
+        ways(dy, dx, remote(dsend.at[(1 + dy) // 2], cdrecv.at[(1 - dy) + (1 - dx) // 2, ngz:], send_cd, h_recv.at[5], at(dy, dx)))
 
 
     layer_of_lane = lax.rem(lane8[0:1], 2 * nz) // 2
@@ -315,6 +321,11 @@
     raw_corner(-1, -1)
     raw_corner(-1, 1)
     signal_peers(far.at[0])
+    for side in range(2):
+        for i in range(2):
+            swsend[side, i] = swapped(dsend[side, i])
+    for dy in (-1, 1):
+        ways(dy, 0, remote(swsend.at[(1 + dy) // 2], cyrecv.at[(1 - dy) // 2, ngz * PLANES:], send_cy, h_recv.at[5], at(dy, 0)))
 
     def tile_of(g):
         return slice(g * HALO, (g + 1) * HALO)
@@ -391,17 +402,16 @@
                                         {"gx": ix + dx, "gy": iy + dy, "gz": lax.rem(iz + d, ngz)})) for d in parts]
 
     def corner_strips(dy, dx, parts):
-        start(to_all(dy, dx, strips.at[0 if dy < 0 else last_head], cdrecv.at[(1 - dy) + (1 - dx) // 2, iz], send_cd, 3, parts))
+        start(to_all(dy, dx, strips.at[0 if dy < 0 else last_head], cdrecv.at[(1 - dy) + (1 - dx) // 2, iz], send_cd, 1, parts))
 
     pl.semaphore_wait(far.at[0], ngz - 1)
-    pl.semaphore_wait(near.at[2], ngz - 1)
     corner_strips(-1, -1, range(ngz))
     corner_strips(-1, 1, range(ngz))
-    known(3, 0, -1)
+    known(2, 0, -1)
     raw_corner(1, -1)
     corner_strips(1, -1, range(1))
     for dx in (-1, 1):
-        start(to_all(0, dx, strips, cxrecv.at[(1 - dx) // 2, pl.ds(iz * nstrips, nstrips)], send_cx, 2))
+        start(to_all(0, dx, strips, cxrecv.at[(1 - dx) // 2, pl.ds(iz * nstrips, nstrips)], send_cx, 1))
     for dy in (-1, 1):
         start(to_all(dy, 0, ystrips.at[(1 + dy) // 2], cyrecv.at[(1 - dy) // 2, pl.ds(iz * PLANES, PLANES)], send_cy, 1))
 
@@ -557,8 +567,8 @@
     layers_of(solve, 0, most)
 
     corners = beside_y * beside_x
-    wait_many(beside_y + beside_x, [(n, zplanes.at[0, 0:2 * n]) for n in range(1, 5)], send_cx, h_recv.at[5], False)
-    wait_many(corners, ((1, cdrecv.at[0, ngz:]), (2, cdrecv.at[0:2, ngz:]), (4, cdrecv.at[:, ngz:])), send_cd, h_recv.at[6], False)
+    place = 3 * beside_y + beside_x
+    wait_many(place, around(lambda cy, cx: 2 * (cy + cx + cy * cx), False), send_cx, h_recv.at[5], False)
     from_top = raw_group8 < layers
     ours, theirs = [], []
     for i in range(2):
@@ -569,16 +579,19 @@
     pattern = nil8
     for k in range(layers):
         pattern = jnp.where(lax.rem(group8, layers) == (k + raw_lane // (2 * HALO)) % layers, rowk[0, k * HALO:(k + 1) * HALO, :], pattern)
-    both = jnp.where(top8, jnp.sum(t * (ours[0] - theirs[0]), axis=0, keepdims=True),
+    both = jnp.where(lax.rem(row8, 2) == 0, jnp.sum(t * (ours[0] - theirs[0]), axis=0, keepdims=True),
                      jnp.sum(t * pattern, axis=0, keepdims=True))
-    summed = both
-    for k in range(1, layers):
-        summed = summed + pltpu.roll(both, nx - 2 * HALO * k, 1)
-    upper = pltpu.roll(summed, (2 * nx - raw_lane - HALO) % nx, 1)
-    lower = pltpu.roll(summed, (2 * nx - raw_lane - 2 * HALO * layers - HALO) % nx, 1)
-    zplanes[iz, first_part] = jnp.where(row8 < 2, upper, pltpu.roll(lower, 2, 0))
+
+    def unpacked(side):
+        total = None
+        for k in range(layers):
+            moved = pltpu.roll(both, (2 * nx - raw_lane - 2 * HALO * (side * layers + k) - HALO) % nx, 1)
+            total = moved if total is None else total + moved
+        return total
+
+    zplanes[iz, first_part] = jnp.where(row8 < 2, unpacked(0), unpacked(1))
     for side, g in ends:
-        tiles = [swapped(cyrecv[side, ngz * PLANES + i]) for i in range(2)]
+        tiles = [cyrecv[side, ngz * PLANES + i] for i in range(2)]
         there = [jnp.where(even8, cdrecv[2 * side, ngz + i], cdrecv[2 * side + 1, ngz + i]) for i in range(2)]
         face = jnp.where(there[1] > 0.0, 1.0 / (tiles[1] + there[1]), 0.0)
         flux_l, flux_r, weight_l, weight_r = sums_of(face * (tiles[0] - there[0]), face * lanek[0], 0)
@@ -586,17 +599,14 @@
                                   at_sides(flux_r, flux_l), at_sides(weight_r, weight_l))):
             zplanes[iz, first_part + 1 + 4 * side + n] = tile
     for d in range(1, ngz):
-        remote(zplanes.at[iz, first_part:], zplanes.at[iz, first_part:], send_cz, c_recv.at[4],
+        remote(zplanes.at[iz, first_part:], zplanes.at[iz, first_part:], send_cz, c_recv.at[2],
                {"gx": ix, "gy": iy, "gz": lax.rem(iz + d, ngz)}).start()
     layers_of(solve, most, nz)
 
     if ngz > 1:
         others = zplanes.at[0:ngz - 1, 0:first_part]
         remote(others, others, send_cz, c_recv.at[0], z_device(0)).wait_recv()
-    y_early, x_early = slice(0, ngz * PLANES), slice(0, ngz * nstrips)
-    wait_many(beside_y, ((1, cyrecv.at[0, y_early]), (2, cyrecv.at[:, y_early])), send_cy, c_recv.at[1], False)
-    wait_many(beside_x, ((1, cxrecv.at[0, x_early]), (2, cxrecv.at[:, x_early])), send_cx, c_recv.at[2], False)
-    wait_many(corners, ((1, cdrecv.at[0, 0:ngz]), (2, cdrecv.at[0:2, 0:ngz]), (4, cdrecv.at[:, 0:ngz])), send_cd, c_recv.at[3], False)
+    wait_many(place, around(lambda cy, cx: PLANES * cy + nstrips * cx + cy * cx, True), send_cx, c_recv.at[1], False)
 
     def gathered(part):
         total = part(0)
@@ -667,7 +677,7 @@
 
     if ngz > 1:
         rest = zplanes.at[0:ngz - 1, first_part:]
-        remote(rest, rest, send_cz, c_recv.at[4], z_device(0)).wait_recv()
+        remote(rest, rest, send_cz, c_recv.at[2], z_device(0)).wait_recv()
     lines = jnp.where(strip8, gathered(lambda i: zplanes[i, first_part]), 0.0)
     beyond(b, lines)
     for side, t, here in ((0, 1, top8), (1, groups, bottom8)):
@@ -777,10 +787,10 @@
             vmem(3, nz, nx), vmem(nz + 1, ny, nx), vmem(2, ey, nx),
             vmem(ngz, PLANES * groups + 1 + strips + 9, HALO, nx), vmem(2, PLANES, HALO, nx), vmem(strips, HALO, nx),
             vmem(2, ngz * PLANES + 2, HALO, nx), vmem(2, ngz * strips + 2, HALO, nx), vmem(4, ngz + 2, HALO, nx),
-            vmem(2, HALO, nx), vmem(2, 2, HALO, nx), vmem(2, 4, nz, nx), vmem(2, 2, ey + 2 * HALO, nx),
+            vmem(2, HALO, nx), vmem(2, 2, HALO, nx), vmem(2, 2, HALO, nx), vmem(2, 4, nz, nx), vmem(2, 2, ey + 2 * HALO, nx),
             pltpu.SMEM((nz,), facies.dtype), pltpu.SMEM((3, facets, 3), f32), pltpu.SMEM((3, facets, 3), f32),
             pltpu.SMEM((NCOEF, facets), f32),
-            pltpu.SemaphoreType.REGULAR((4,)), pltpu.SemaphoreType.REGULAR((2,)), dma(7), dma(7), dma(5),
+            pltpu.SemaphoreType.REGULAR((3,)), pltpu.SemaphoreType.REGULAR((2,)), dma(7), dma(6), dma(3),
         ],
         compiler_params=pltpu.CompilerParams(collective_id=0, has_side_effects=True, vmem_limit_bytes=limit),
         name="cpr_apply",

time: 11.4 us -> 11.3 us (level)
  the two profiles are of different devices: /device:TPU:1 before, /device:TPU:0 now
where the time goes in v6:
time: 11.3 us; the launch traced here: 11.1 us
  Pallas kernels  10.4 us (92%)
  between operations  0.64 us (6%)
    pallas_call x1, Pallas kernels, per_device(): pl.pallas_call(functools.partial(kernel, sizes), out_shape=(vmem(3, *cell...  9.4 us
    pallas_call x1, Pallas kernels, per_device(): pl.pallas_call(functools.partial(finish_kernel, parts), out_shape=(jax.Sh...  1.05 us

profile of v6, /device:TPU:0, one launch (start us, length us, event | category | flops | bytes accessed | tf_op | source)
XLA Modules:
  0.0 11.1 jit_solution(137810711742434657)
XLA Ops:
  0.6 9.4 %cpr_apply.1 = (f32[3,16,40,128]{3,2,1,0:T(8,128)S(1)}, f32[3,16,40,128]{3,2,1,0:T(8,128)S(1)}, f32[16,40,128]{2,1,0:T(8,128)S(1)}, f32[16,56,128]{2,1,0:T(8,128...) custom-call(s32[16]{0:T(128)} %facies_hbm.1, f32[3,4,3]{2,1,0:T(4,128)} %bitcast.2, ...), custom_call_target="tpu_custom_call" | custom-call | tf_op jit(solution)/shard_map/cpr_apply/pallas_call | solution.py:776
  10.0 1.0 %cpr_finish.1 = (f32[3,16,40,128]{3,2,1,0:T(8,128)}, f32[40,128]{1,0:T(8,128)}) custom-call(f32[3,16,40,128]{3,2,1,0:T(8,128)S(1)} %get-tuple-element.9.w, f32[3,16,40,128]{3,2,1,0:T(8,128)S(1)} %get-tuple-element.10.qv, f32[16,40,128]{2,1,0:T(8,128)S(1)} %get-tuple-element.11.tzs, f32[16,56,128]{2,1,0:T(8,128)S(1)} %get-tuple-element.12.ty, ...), custom_call_target="tpu_custom_call" | custom-call | tf_op jit(solution)/shard_map/cpr_finish/pallas_call | solution.py:800

commit v7 on v6

--- a/solution.py
+++ b/solution.py
@@ -317,15 +317,15 @@
     loads[2].wait()
     loads[3].wait()
 
-    known(0, -1, 0)
-    raw_corner(-1, -1)
-    raw_corner(-1, 1)
-    signal_peers(far.at[0])
     for side in range(2):
         for i in range(2):
             swsend[side, i] = swapped(dsend[side, i])
     for dy in (-1, 1):
         ways(dy, 0, remote(swsend.at[(1 + dy) // 2], cyrecv.at[(1 - dy) // 2, ngz * PLANES:], send_cy, h_recv.at[5], at(dy, 0)))
+    known(0, -1, 0)
+    raw_corner(-1, -1)
+    raw_corner(-1, 1)
+    signal_peers(far.at[0])
 
     def tile_of(g):
         return slice(g * HALO, (g + 1) * HALO)

time: 11.3 us -> 11.4 us (level)
  the two profiles are of different devices: /device:TPU:0 before, /device:TPU:1 now
where the time goes in v7:
time: 11.4 us; the launch traced here: 11.2 us
  Pallas kernels  10.6 us (93%)
  between operations  0.64 us (6%)
    pallas_call x1, Pallas kernels, per_device(): pl.pallas_call(functools.partial(kernel, sizes), out_shape=(vmem(3, *cell...  9.51 us
    pallas_call x1, Pallas kernels, per_device(): pl.pallas_call(functools.partial(finish_kernel, parts), out_shape=(jax.Sh...  1.05 us

profile of v7, /device:TPU:1, one launch (start us, length us, event | category | flops | bytes accessed | tf_op | source)
XLA Modules:
  0.0 11.2 jit_solution(8900884484413828838)
XLA Ops:
  0.6 9.5 %cpr_apply.1 = (f32[3,16,40,128]{3,2,1,0:T(8,128)S(1)}, f32[3,16,40,128]{3,2,1,0:T(8,128)S(1)}, f32[16,40,128]{2,1,0:T(8,128)S(1)}, f32[16,56,128]{2,1,0:T(8,128...) custom-call(s32[16]{0:T(128)} %facies_hbm.1, f32[3,4,3]{2,1,0:T(4,128)} %bitcast.2, ...), custom_call_target="tpu_custom_call" | custom-call | tf_op jit(solution)/shard_map/cpr_apply/pallas_call | solution.py:776
  10.2 1.0 %cpr_finish.1 = (f32[3,16,40,128]{3,2,1,0:T(8,128)}, f32[40,128]{1,0:T(8,128)}) custom-call(f32[3,16,40,128]{3,2,1,0:T(8,128)S(1)} %get-tuple-element.9.w, f32[3,16,40,128]{3,2,1,0:T(8,128)S(1)} %get-tuple-element.10.qv, f32[16,40,128]{2,1,0:T(8,128)S(1)} %get-tuple-element.11.tzs, f32[16,56,128]{2,1,0:T(8,128)S(1)} %get-tuple-element.12.ty, ...), custom_call_target="tpu_custom_call" | custom-call | tf_op jit(solution)/shard_map/cpr_finish/pallas_call | solution.py:800
